TPU v7x, 128 devices: a whole 4x4x4 slice. The times are simulated.
128 devices in a mesh: samp: 8 (over x, y_hi), probe: 16 (over y_lo, z, core).
Axes of the slice: x: 4, y: 4 (y_hi: 2, y_lo: 2; y = y_hi * 2 + y_lo), z: 4, core: 2. Of those that a mesh axis runs over, the one named last changes fastest.
Arguments:
- methyl: bfloat16 [8192, 32768], P('samp', 'probe'), may hold values from -0.25 to 1.25
- atlas: bfloat16 [64, 32768], P(None, 'probe'), may hold values from 0 to 1, as said below
- panel_ids: int32 [64], replicated, may hold values from 0 to 63, each once
Outputs:
- relmat: float32 [3, 8192, 1024], P(None, 'samp', 'probe')
- scores: float32 [32, 8192], P(None, ('samp', 'probe'))
Inputs may be any that keep to these rules, and one draw needn't show every extreme that they name: atlas values are beta values between 0 and 1.
All inputs are finite; a program needn't handle non-finite values.
Results may differ from a plain program's by a relative error of at most 0.003.
Values may be sent and summed in bfloat16 or wider, within the bound.
A program may use at most 128 MiB of HBM per device.

v0:
```python
import jax
import jax.numpy as jnp
from jax import lax
from jax.sharding import PartitionSpec as P

K = 32
ITERS = 128


def shifted(value, axis, by):
    peers = lax.axis_size(axis)
    return lax.ppermute(value, axis, [(i, (i + by) % peers) for i in range(peers)])


def ridge_solve(wgram, cross, ridge):
    eye = jnp.eye(wgram.shape[0], dtype=wgram.dtype)
    factor = jnp.linalg.cholesky(wgram + ridge * eye)
    middle = lax.linalg.triangular_solve(factor, cross, left_side=True, lower=True)
    return lax.linalg.triangular_solve(factor, middle, left_side=True, lower=True, transpose_a=True)


def nnls_steps(gram, proj):
    step_rate = 1.0 / jnp.trace(gram)

    def descend(turn_index, weights):
        grad_term = jnp.dot(gram, weights, precision=lax.Precision.HIGHEST) - proj
        return jnp.maximum(weights - step_rate * grad_term, 0.0)

    return lax.fori_loop(0, ITERS, descend, jnp.full(proj.shape, 1.0 / K, jnp.float32))


def tile_product(first_block, other_block):
    return lax.dot_general(
        first_block, other_block, (((1,), (1,)), ((), ())), preferred_element_type=jnp.float32
    )


def body(methyl, atlas, panel_ids):
    samples = methyl.shape[0] * lax.axis_size("samp")
    probes = methyl.shape[1] * lax.axis_size("probe")
    share_width = methyl.shape[0] // lax.axis_size("probe")
    selector = (panel_ids[:K, None] == jnp.arange(atlas.shape[0], dtype=jnp.int32)[None, :]).astype(
        jnp.bfloat16
    )
    panel = jnp.dot(selector, atlas, preferred_element_type=jnp.float32).astype(jnp.bfloat16)
    gram_part = jnp.dot(panel, panel.T, preferred_element_type=jnp.float32)
    proj_part = lax.dot_general(
        panel, methyl, (((1,), (1,)), ((), ())), preferred_element_type=jnp.float32
    )
    gram, proj = lax.psum((gram_part, proj_part), "probe")
    weights = nnls_steps(gram, proj)
    start = lax.axis_index("probe") * share_width
    scores = K * lax.dynamic_slice_in_dim(weights, start, share_width, 1)
    design = weights.astype(jnp.bfloat16)
    cross_part = jnp.dot(design, methyl, preferred_element_type=jnp.float32)
    wgram_part = jnp.dot(design, design.T, preferred_element_type=jnp.float32)
    design_wide = design.astype(jnp.float32)
    cross, wgram = lax.psum((cross_part, wgram_part), "samp")
    loadings = ridge_solve(wgram, cross, 0.0001 * samples)
    fitted = lax.dot_general(
        design_wide, loadings, (((0,), (0,)), ((), ())), precision=lax.Precision.HIGHEST
    )
    residual = methyl.astype(jnp.float32) - fitted
    spread = lax.psum(jnp.sum(residual * residual, axis=0), "samp")
    zscore = (residual * lax.rsqrt(spread / samples + 1e-06)).astype(jnp.bfloat16)
    before = shifted(zscore, "samp", 1)
    after = shifted(zscore, "samp", -1)
    tile_terms = jnp.stack(
        [tile_product(zscore, zscore), tile_product(zscore, before), tile_product(zscore, after)]
    )
    tile_totals = lax.psum_scatter(tile_terms, "probe", scatter_dimension=2, tiled=True)
    return (tile_totals / probes, scores)


def solution(mesh):
    placed = (P("samp", "probe"), P(None, "probe"), P())
    return jax.shard_map(
        body,
        mesh=mesh,
        in_specs=placed,
        out_specs=(P(None, "samp", "probe"), P(None, ("samp", "probe"))),
        check_vma=False,
    )
```

profile of v0, /device:TPU:1, one launch (start us, length us, event | category | flops | bytes accessed | tf_op | source)
XLA Modules:
  0.0 860.1 jit_solution(3452376709186517423)
XLA Ops:
  9.0 4.2 fusion.21
  13.4 54.3 %psum.35 = f32[32,32]{1,0:T(8,128)S(1)} all-reduce(f32[32,32]{1,0:T(8,128)S(1)} %fusion.20), channel_id=1, replica_groups=mesh['samp'=8,'probe'=16] {'probe'}, use_global_device_ids=true, to_apply=%region_0.0 | all-reduce | flops 1024 | bytes 8192 | tf_op jit(solution)/shard_map/psum | solution.py:50
  68.9 63.3 %all-reduce.5.cloned.1.call-done = f32[32,1024]{1,0:T(8,128)} async-done(((f32[32,1024]{1,0:T(8,128)}), f32[32,1024]{1,0:T(8,128)}) %all-reduce.5.cloned.1.call-update) | async-done | bytes 131088 | tf_op jit(solution)/shard_map/psum | solution.py:50
  132.3 155.7 %while.11 = (s32[]{:T(128)}, f32[32,1024]{1,0:T(8,128)S(1)}, f32[]{:T(128)}, f32[32,32]{1,0:T(8,128)S(1)}, f32[32,1024]{1,0:T(8,128)}, /*index=5*/s32[]{:T(128)}, s32[]{:T(128)}) while((s32[]{:T(128)}, f32[32,1024]{1,0:T(8,128)S(1)}, f32[]{:T(128)}, f32[32,32]{1,0:T(8,128)S(1)}, f32[32,1024]{1,0:T(8,128)}, /*index=5*/s32[]{:T(128)}, ...), condition=%wide.region_4.5_spmd.clone, body=%wide.region_3.4_spmd.clone.sunk | while | flops 12779523 | bytes 659547 | solution.py:29
  134.7 1.2 fusion.43
  138.3 1.2 fusion.43
  139.6 1.2 fusion.43
  143.2 1.2 fusion.43
  146.9 1.2 fusion.43
  149.3 1.2 fusion.43
  151.7 1.2 fusion.43
  157.8 1.2 fusion.43
  160.2 1.2 fusion.43
  165.1 1.2 fusion.43
  166.3 1.2 fusion.43
  168.8 1.2 fusion.43
  173.6 1.2 fusion.43
  177.3 1.2 fusion.43
  180.9 1.2 fusion.43
  185.8 1.2 fusion.43
  189.4 1.2 fusion.43
  191.9 1.2 fusion.43
  194.3 1.2 fusion.43
  200.4 1.2 fusion.43
  202.8 1.2 fusion.43
  207.7 1.2 fusion.43
  211.3 1.2 fusion.43
  216.2 1.2 fusion.43
  219.8 1.2 fusion.43
  223.5 1.2 fusion.43
  228.3 1.2 fusion.43
  232.0 1.2 fusion.43
  234.4 1.2 fusion.43
  236.9 1.2 fusion.43
  242.9 1.2 fusion.43
  245.4 1.2 fusion.43
  250.2 1.2 fusion.43
  253.9 1.2 fusion.43
  257.5 1.2 fusion.43
  258.8 1.2 fusion.43
  262.4 1.2 fusion.43
  266.0 1.2 fusion.43
  270.9 1.2 fusion.43
  279.4 1.2 fusion.43
  288.0 3.7 fusion.16
  291.8 34.1 %psum.37 = f32[32,32]{1,0:T(8,128)S(1)} all-reduce(f32[32,32]{1,0:T(8,128)S(1)} %fusion.18), channel_id=1, replica_groups=mesh['samp'=8,'probe'=16] {'samp'}, use_global_device_ids=true, to_apply=%region_5.6 | all-reduce | flops 1024 | bytes 8192 | tf_op jit(solution)/shard_map/psum | solution.py:58
  326.0 2.9 cholesky.13
  330.3 2.4 custom-call.8
  332.8 76.1 %all-reduce.7.cloned.1.call-done = f32[32,2048]{1,0:T(8,128)} async-done(((f32[32,2048]{1,0:T(8,128)}), f32[32,2048]{1,0:T(8,128)}) %all-reduce.7.cloned.1.call-update) | async-done | bytes 262160 | tf_op jit(solution)/shard_map/psum | solution.py:58
  408.9 1.4 fusion.10
  410.6 7.9 multiply_reduce_fusion
  418.6 17.1 %psum.39 = f32[2048]{0:T(1024)S(1)} all-reduce(f32[2048]{0:T(1024)S(1)} %get-tuple-element.62), channel_id=1, replica_groups=mesh['samp'=8,'probe'=16] {'samp'}, use_global_device_ids=true, to_apply=%region_10.11 | all-reduce | flops 2048 | bytes 16384 | tf_op jit(solution)/shard_map/psum | solution.py:64
  435.7 6.1 multiply_convert_fusion
  441.7 1.6 collective-permute-start.1
  443.4 1.4 collective-permute-start
  444.8 4.5 convolution_bitcast_fusion.2
  449.3 172.6 %collective-permute-done.1 = bf16[1024,2048]{1,0:T(8,128)(2,1)S(1)} collective-permute-done((bf16[1024,2048]{1,0:T(8,128)(2,1)S(1)}, bf16[1024,2048]{1,0:T(8,128)(2,1)S(1)}, u32[]{:S(2)}, u32[]{:S(2)}) %collective-permute-start.1) | collective-permute-done | bytes 4194336 | tf_op jit(solution)/shard_map/ppermute | solution.py:12
  621.9 4.7 convolution_bitcast_fusion
  626.6 4.7 convolution_bitcast_fusion.1
  631.3 5.2 pad_maximum_fusion
  636.5 18.4 %copy.8 = f32[3,1024,1024]{1,0,2:T(4,128)} copy(f32[3,1024,1024]{2,1,0:T(8,128)} %pad_maximum_fusion) | data formatting | bytes 25165824 | tf_op jit(solution)/shard_map/stack | solution.py:68
  657.5 193.2 %all-reduce.9.cloned.1.call-done = f32[3,1024,1024]{1,0,2:T(4,128)} async-done(((f32[3,1024,1024]{1,0,2:T(4,128)}), f32[3,1024,1024]{1,0,2:T(4,128)}) %all-reduce.9.cloned.1.call-update) | async-done | bytes 12582928
  850.7 1.5 dynamic-slice_multiply_fusion
  852.2 1.3 copy.9
  (244 shorter events, 111.0 us)
Async XLA Ops:
  7.2 1.0 copy-start
  7.2 125.1 %all-reduce.5.cloned.1.call-start = ((), (), s32[]{:S(2)}) async-start(), calls=%async_computation | async-start | bytes 262144 | tf_op jit(solution)/shard_map/psum | solution.py:50
  13.2 395.7 %all-reduce.7.cloned.1.call-start = ((), (), s32[]{:S(2)}) async-start(), calls=%async_computation.1 | async-start | bytes 524288 | tf_op jit(solution)/shard_map/psum | solution.py:58
  329.0 521.8 %all-reduce.9.cloned.1.call-start = ((), (), s32[]{:S(2)}) async-start(), calls=%async_computation.2 | async-start | bytes 33554432
  441.7 180.2 %collective-permute-start.1 = (bf16[1024,2048]{1,0:T(8,128)(2,1)S(1)}, bf16[1024,2048]{1,0:T(8,128)(2,1)S(1)}, u32[]{:S(2)}, u32[]{:S(2)}) collective-permute-start(bf16[1024,2048]{1,0:T(8,128)(2,1)S(1)} %multiply_convert_fusion), channel_id=1, source_target_pairs={{0,112},{16,0},{32,16},{48,32},{64,48},{80,64},{96,80},{112,96},{1... | collective-permute-start | bytes 12582920 | tf_op jit(solution)/shard_map/ppermute | solution.py:12
  443.4 183.2 %collective-permute-start = (bf16[1024,2048]{1,0:T(8,128)(2,1)S(1)}, bf16[1024,2048]{1,0:T(8,128)(2,1)S(1)}, u32[]{:S(2)}, u32[]{:S(2)}) collective-permute-start(bf16[1024,2048]{1,0:T(8,128)(2,1)S(1)} %multiply_convert_fusion), channel_id=1, source_target_pairs={{0,16},{16,32},{32,48},{48,64},{64,80},{80,96},{96,112},{112,0},{1... | collective-permute-start | bytes 12582920 | tf_op jit(solution)/shard_map/ppermute | solution.py:12
  654.9 0.7 copy-start.2
  655.0 198.6 %copy-start.1 = (bf16[64,2048]{1,0:T(8,128)(2,1)S(1)}, bf16[64,2048]{1,0:T(8,128)(2,1)}, u32[]{:S(2)}) copy-start(bf16[64,2048]{1,0:T(8,128)(2,1)} %param.6) | copy-start | bytes 786436
Sparse Core Ops, SparseCore 0:
  13.3 118.8 all-reduce.4
  329.1 79.7 all-reduce.6
  655.1 195.6 all-reduce.8
where the time goes:
time: 864 us; the launch traced here: 860 us
  waiting for transfers between devices  505 us (58%)
  matrix products  183 us (21%)
  blocking collectives  106 us (12%)
  local copies, waits for them, and re-layouts  23.3 us (3%)
  other arithmetic  20.7 us (2%)
  between operations  15.1 us (2%)
    unnamed x4, waiting for transfers between devices  193 us
    ppermute x2, waiting for transfers between devices, shifted(): lax.ppermute(value, axis, [(i, (i + by) % peers) for i in range(peers)])  173 us
    dot_general x128, matrix products, descend(): grad_term = jnp.dot(gram, weights, precision=lax.Precision.HIGHEST) - proj  150 us
    psum x1, waiting for transfers between devices, body(): cross, wgram = lax.psum((cross_part, wgram_part), 'samp')  76.1 us
    psum x1, waiting for transfers between devices, body(): gram, proj = lax.psum((gram_part, proj_part), 'probe')  63.3 us
    psum x1, blocking collectives, body(): gram, proj = lax.psum((gram_part, proj_part), 'probe')  54.3 us
    psum x1, blocking collectives, body(): cross, wgram = lax.psum((cross_part, wgram_part), 'samp')  34.1 us
    another operation x1, local copies, waits for them, and re-layouts, body(): jnp.stack([tile_product(zscore, zscore), tile_product(zscore, before), ti...  18.4 us
  transfers between devices with their start and end apart: 5, of which 4 were waited for; matrix products, arithmetic and copies ran while one was open for 2% of the time, Pallas kernels for 0%

commit v1 on v0

v1 whole, which is shorter than its diff:
```python
import functools

import jax
import jax.numpy as jnp
from jax import lax
from jax.experimental import pallas as pl
from jax.experimental.pallas import tpu as pltpu
from jax.sharding import PartitionSpec as P

K = 32
ITERS = 128
MESH = pl.DeviceIdType.MESH
F32 = jnp.float32
BF16 = jnp.bfloat16


def dot(a, b, dims=((1,), (0,))):
    return lax.dot_general(a, b, (dims, ((), ())), preferred_element_type=F32)


def copy_to(src, dst, send_sem, recv_sem, axis, peer):
    return pltpu.make_async_remote_copy(
        src_ref=src, dst_ref=dst, send_sem=send_sem, recv_sem=recv_sem,
        device_id={axis: peer}, device_id_type=MESH,
    )


def exchange_start(src_of, dst, send_sem, recv_sem, axis, peers, me):
    def body(step, carry):
        peer = lax.rem(me + step, peers)
        copy_to(src_of(peer), dst.at[me], send_sem.at[peer], recv_sem.at[me], axis, peer).start()
        return carry
    lax.fori_loop(1, peers, body, 0)


def exchange_wait(src_of, dst, send_sem, recv_sem, axis, peers, me):
    def body(step, carry):
        peer = lax.rem(me + step, peers)
        copy = copy_to(src_of(peer), dst.at[peer], send_sem.at[peer], recv_sem.at[peer], axis, peer)
        copy.wait_recv()
        copy.wait_send()
        return carry
    lax.fori_loop(1, peers, body, 0)


def split3(value):
    high = value.astype(BF16)
    rest = value - high.astype(F32)
    mid = rest.astype(BF16)
    low = (rest - mid.astype(F32)).astype(BF16)
    return high, mid, low


def chain_kernel(
    samps, probes_n, samples,
    methyl, atlas, ids, scores, zout, dout,
    pmsg, prcv, gcol, dmsg, drcv, cmsg, crcv, lmsg, lrcv, resid, smsg, srcv, lsplit,
    psem, prsem, dsem, drsem, csem, crsem, lsem, lrsem, ssem, srsem,
):
    me_p = lax.axis_index("probe")
    me_s = lax.axis_index("samp")
    rows, cols = methyl.shape
    share = rows // probes_n
    width = cols // samps

    barrier = pltpu.get_barrier_semaphore()

    def greet(axis, peers, me):
        def body(step, carry):
            pl.semaphore_signal(
                barrier, inc=1, device_id={axis: lax.rem(me + step, peers)}, device_id_type=MESH
            )
            return carry
        lax.fori_loop(1, peers, body, 0)
    greet("probe", probes_n, me_p)
    greet("samp", samps, me_s)

    kinds = atlas.shape[0]
    select_t = (lax.broadcasted_iota(jnp.int32, (kinds, kinds), 0) == ids[...]).astype(F32)
    selector = select_t.T[:K].astype(BF16)
    panel = dot(selector, atlas[...]).astype(BF16)
    gram_part = dot(panel, panel, ((1,), (1,)))
    pad = jnp.zeros((K, 128 - share - K), F32)

    def project(step, carry):
        block = methyl[pl.ds(pl.multiple_of(step * 2 * share, 2 * share), 2 * share), :]
        part = dot(panel, block, ((1,), (1,)))
        pmsg[2 * step] = jnp.concatenate([part[:, :share], gram_part, pad], axis=1)
        pmsg[2 * step + 1] = jnp.concatenate([part[:, share:], gram_part, pad], axis=1)
        return carry
    lax.fori_loop(0, probes_n // 2, project, 0)

    pl.semaphore_wait(barrier, probes_n - 1 + samps - 1)
    from_p = lambda peer: pmsg.at[peer]
    exchange_start(from_p, prcv, psem, prsem, "probe", probes_n, me_p)
    prcv[me_p] = pmsg[me_p]
    exchange_wait(from_p, prcv, psem, prsem, "probe", probes_n, me_p)
    total = prcv[0]
    for peer in range(1, probes_n):
        total = total + prcv[peer]
    gram = total[:, share:share + K]
    proj = total[:, :share]

    diag = lax.broadcasted_iota(jnp.int32, (K, K), 0) == lax.broadcasted_iota(jnp.int32, (K, K), 1)
    trace = jnp.sum(jnp.where(diag, gram, 0.0), axis=(0, 1), keepdims=True)
    rate = 1.0 / trace
    scaled = gram * rate
    half = K // 2
    left_k = lax.broadcasted_iota(jnp.int32, (K, 128), 1) < share
    for k in range(half):
        gcol[k] = jnp.where(
            left_k,
            jnp.broadcast_to(scaled[:, k:k + 1], (K, 128)),
            jnp.broadcast_to(scaled[:, half + k:half + k + 1], (K, 128)),
        )
    goal = jnp.concatenate([proj[:half], proj[half:]], axis=1) * rate
    left = lax.broadcasted_iota(jnp.int32, (half, 128), 1) < share

    def descend(step, state):
        sums = [None, None]
        for k in range(half):
            term = gcol[k] * jnp.broadcast_to(state[k:k + 1, :], (K, 128))
            sums[k % 2] = term if sums[k % 2] is None else sums[k % 2] + term
        acc = sums[0] + sums[1]
        keep = jnp.where(left, acc[:half], acc[half:])
        other = jnp.where(left, acc[half:], acc[:half])
        grad = keep + pltpu.roll(other, share, axis=1) - goal
        return jnp.maximum(state - grad, 0.0)
    state = lax.fori_loop(0, ITERS, descend, jnp.full((half, 128), 1.0 / K, F32))
    weights = jnp.concatenate([state[:, :share], state[:, share:]], axis=0)
    scores[...] = weights * float(K)

    four = jnp.concatenate([weights] * 4, axis=0)
    wide = jnp.concatenate([four, jnp.zeros((4 * K, 128 - share), F32)], axis=1)
    dmsg[...] = wide.T[:share].astype(BF16)
    from_d = lambda peer: dmsg
    exchange_start(from_d, drcv, dsem, drsem, "probe", probes_n, me_p)
    drcv[me_p] = dmsg[...]
    exchange_wait(from_d, drcv, dsem, drsem, "probe", probes_n, me_p)
    design4 = drcv[...].reshape(rows, 4 * K)
    dout[...] = design4
    design = design4.astype(F32).T[:K].astype(BF16)

    wgram_part = dot(design, design, ((1,), (1,)))
    wpad = jnp.concatenate([wgram_part, jnp.zeros((K, 128 - K), F32)], axis=1)

    def crossing(step, carry):
        block = methyl[:, pl.ds(pl.multiple_of(step * width, width), width)]
        cmsg[step] = jnp.concatenate([dot(design, block), wpad], axis=1)
        return carry
    lax.fori_loop(0, samps, crossing, 0)
    from_c = lambda peer: cmsg.at[peer]
    exchange_start(from_c, crcv, csem, crsem, "samp", samps, me_s)
    crcv[me_s] = cmsg[me_s]
    exchange_wait(from_c, crcv, csem, crsem, "samp", samps, me_s)
    both = crcv[0]
    for peer in range(1, samps):
        both = both + crcv[peer]

    matrix = both[:, width:]
    row_id = lax.broadcasted_iota(jnp.int32, (K, 128), 0)
    lane_id = lax.broadcasted_iota(jnp.int32, (K, 128), 1)
    matrix = matrix + jnp.where(row_id == lane_id, 0.0001 * samples, 0.0)
    right = both[:, :width]
    row_w = lax.broadcasted_iota(jnp.int32, (K, 1), 0)
    for k in range(K):
        column = matrix[:, k:k + 1]
        pivot = 1.0 / matrix[k:k + 1, k:k + 1]
        factor = jnp.where(row_w == k, 0.0, column * pivot)
        matrix_row = matrix[k:k + 1, :]
        right_row = right[k:k + 1, :]
        matrix = matrix - factor * matrix_row
        right = right - factor * right_row
    pivots = jnp.sum(jnp.where(row_id == lane_id, matrix, 0.0), axis=1, keepdims=True)
    lmsg[...] = right / pivots
    from_l = lambda peer: lmsg
    exchange_start(from_l, lrcv, lsem, lrsem, "samp", samps, me_s)
    lrcv[me_s] = lmsg[...]
    exchange_wait(from_l, lrcv, lsem, lrsem, "samp", samps, me_s)

    def residue(step, carry):
        high, mid, low = split3(lrcv[step])
        stacked = jnp.concatenate([high, mid, low, jnp.zeros_like(low)], axis=0)
        at = pl.ds(pl.multiple_of(step * width, width), width)
        lsplit[:, at] = stacked
        sums = jnp.zeros((1, width), F32)
        for r in range(0, rows, 256):
            res = methyl[r:r + 256, at].astype(F32) - dot(drcv_rows(drcv, r, 256), stacked)
            resid[r:r + 256, at] = res
            sums = sums + jnp.sum(res * res, axis=0, keepdims=True)
        smsg[:, at] = sums
        return carry

    def drcv_rows(ref, start, count):
        return ref[start // share:(start + count) // share].reshape(count, 4 * K)
    lax.fori_loop(0, samps, residue, 0)
    from_s = lambda peer: smsg
    exchange_start(from_s, srcv, ssem, srsem, "samp", samps, me_s)
    srcv[me_s] = smsg[...]
    exchange_wait(from_s, srcv, ssem, srsem, "samp", samps, me_s)
    spread = srcv[0]
    for peer in range(1, samps):
        spread = spread + srcv[peer]
    smsg[...] = lax.rsqrt(spread * (1.0 / samples) + 1e-06)

    def normalize(step, carry):
        at = pl.ds(pl.multiple_of(step * width, width), width)
        zout[:, at] = (resid[:, at] * smsg[:, at]).astype(BF16)
        return carry
    lax.fori_loop(0, samps, normalize, 0)


def chain(mesh, methyl, atlas, panel_ids):
    samps, probes_n = mesh.shape["samp"], mesh.shape["probe"]
    rows, cols = methyl.shape
    share, width = rows // probes_n, cols // samps
    vmem = pl.BlockSpec(memory_space=pltpu.VMEM)
    dma = pltpu.SemaphoreType.DMA
    return pl.pallas_call(
        functools.partial(chain_kernel, samps, probes_n, rows * samps),
        out_shape=(
            jax.ShapeDtypeStruct((K, share), F32),
            jax.ShapeDtypeStruct((rows, cols), BF16),
            jax.ShapeDtypeStruct((rows, 4 * K), BF16),
        ),
        in_specs=[vmem] * 3,
        out_specs=(vmem,) * 3,
        scratch_shapes=[
            pltpu.VMEM((probes_n, K, 128), F32),
            pltpu.VMEM((probes_n, K, 128), F32),
            pltpu.VMEM((K // 2, K, 128), F32),
            pltpu.VMEM((share, 4 * K), BF16),
            pltpu.VMEM((probes_n, share, 4 * K), BF16),
            pltpu.VMEM((samps, K, width + 128), F32),
            pltpu.VMEM((samps, K, width + 128), F32),
            pltpu.VMEM((K, width), F32),
            pltpu.VMEM((samps, K, width), F32),
            pltpu.VMEM((rows, cols), F32),
            pltpu.VMEM((1, cols), F32),
            pltpu.VMEM((samps, 1, cols), F32),
            pltpu.VMEM((4 * K, cols), BF16),
            dma((probes_n,)), dma((probes_n,)), dma((probes_n,)), dma((probes_n,)),
            dma((samps,)), dma((samps,)), dma((samps,)), dma((samps,)), dma((samps,)), dma((samps,)),
        ],
        compiler_params=pltpu.CompilerParams(
            collective_id=0, has_side_effects=True, vmem_limit_bytes=48 * 1024 * 1024
        ),
        name="chain",
    )(methyl, atlas, panel_ids.reshape(1, -1))


def shifted(value, axis, by):
    peers = lax.axis_size(axis)
    return lax.ppermute(value, axis, [(i, (i + by) % peers) for i in range(peers)])


def tile_product(first_block, other_block):
    return dot(first_block, other_block, ((1,), (1,)))


def solution(mesh):
    def body(methyl, atlas, panel_ids):
        probes = methyl.shape[1] * mesh.shape["probe"]
        scores, zscore, design = chain(mesh, methyl, atlas, panel_ids)
        before = shifted(zscore, "samp", 1)
        after = shifted(zscore, "samp", -1)
        tile_terms = jnp.stack(
            [tile_product(zscore, zscore), tile_product(zscore, before), tile_product(zscore, after)]
        )
        tile_totals = lax.psum_scatter(tile_terms, "probe", scatter_dimension=2, tiled=True)
        return (tile_totals / probes, scores)

    return jax.shard_map(
        body,
        mesh=mesh,
        in_specs=(P("samp", "probe"), P(None, "probe"), P()),
        out_specs=(P(None, "samp", "probe"), P(None, ("samp", "probe"))),
        check_vma=False,
    )
```

time: 864 us -> 490 us (0.57)
  matrix products: 183 us -> 13.9 us
  waiting for transfers between devices: 505 us -> 365 us
  blocking collectives: 106 us -> 0 us
  Pallas kernels: 0 us -> 60.3 us
  other arithmetic: 20.7 us -> 6.69 us
    dot_general x137 -> x3, matrix products: 181 us -> 13.9 us  [dot(): return lax.dot_general(a, b, (dims, ((), ())), preferred_element_type=F32)]
    psum x2 -> x0, waiting for transfers between devices: 139 us -> none  [the longest x1 76.1 us: body(): cross, wgram = lax.psum((cross_part, wgram_part), 'samp')]
    psum x3 -> x0, blocking collectives: 106 us -> none  [the longest x1 54.3 us: body(): gram, proj = lax.psum((gram_part, proj_part), 'probe')]
    pallas_call x0 -> x1, Pallas kernels: none -> 60.3 us  [chain(): pl.pallas_call(functools.partial(chain_kernel, samps, probes_n, rows * sa...]
    unnamed x4 -> x2, waiting for transfers between devices: 193 us -> 196 us
  transfers between devices with their start and end apart: 5 -> 3, of which waited for: 4 -> 3; matrix products, arithmetic and copies ran while one was open for 2% -> 2% of each run, Pallas kernels for 0% -> 0%
where the time goes in v1:
time: 490 us; the launch traced here: 489 us
  waiting for transfers between devices  365 us (74%)
  Pallas kernels  60.3 us (12%)
  local copies, waits for them, and re-layouts  23.1 us (5%)
  between operations  14.7 us (3%)
  matrix products  13.9 us (3%)
  other arithmetic  6.69 us (1%)
  starting transfers between devices  5.19 us (1%)
    unnamed x2, waiting for transfers between devices  196 us
    ppermute x2, waiting for transfers between devices, shifted(): lax.ppermute(value, axis, [(i, (i + by) % peers) for i in range(peers)])  169 us
    pallas_call x1, Pallas kernels, chain(): pl.pallas_call(functools.partial(chain_kernel, samps, probes_n, rows * sa...  60.3 us
    another operation x1, local copies, waits for them, and re-layouts, body(): jnp.stack([tile_product(zscore, zscore), tile_product(zscore, before), ti...  18.4 us
    dot_general x3, matrix products, dot(): return lax.dot_general(a, b, (dims, ((), ())), preferred_element_type=F32)  13.9 us
  transfers between devices with their start and end apart: 3, of which 3 were waited for; matrix products, arithmetic and copies ran while one was open for 2% of the time, Pallas kernels for 0%

profile of v1, /device:TPU:1, one launch (start us, length us, event | category | flops | bytes accessed | tf_op | source)
XLA Modules:
  0.0 488.5 jit_solution(13380213667259625142)
XLA Ops:
  7.2 0.0 all-reduce.3.cloned.1.call-start
  7.2 0.0 copy-start
  7.2 0.9 copy-done
  8.2 0.0 copy-start.1
  8.2 0.7 copy-done.1
  8.8 60.3 %chain.1 = (f32[32,64]{1,0:T(8,128)S(1)}, bf16[1024,2048]{1,0:T(8,128)(2,1)S(1)}, bf16[1024,128]{1,0:T(8,128)(2,1)}) custom-call(bf16[1024,2048]{1,0:T(8,128)(2,1)} %methyl.1, bf16[64,2048]{1,0:T(8,128)(2,1)S(1)} %copy-done, s32[1,64]{1,0:T(1,128)S(1)} %bitcast.14), custom_call_target="tpu_custom_call" | custom-call | tf_op jit(solution)/shard_map/chain/pallas_call | solution.py:219
  69.1 0.7 collective-permute-start
  69.8 4.4 collective-permute-start.1
  74.3 4.5 convolution_bitcast_fusion.2
  78.8 168.5 %collective-permute-done = bf16[1024,2048]{1,0:T(8,128)(2,1)S(1)} collective-permute-done((bf16[1024,2048]{1,0:T(8,128)(2,1)S(1)}, bf16[1024,2048]{1,0:T(8,128)(2,1)S(1)}, u32[]{:S(2)}, u32[]{:S(2)}) %collective-permute-start) | collective-permute-done | bytes 4194336 | tf_op jit(solution)/shard_map/ppermute | solution.py:254
  247.3 4.7 convolution_bitcast_fusion.1
  252.0 0.2 collective-permute-done.1
  252.2 4.7 convolution_bitcast_fusion
  256.9 5.2 %pad_maximum_fusion = f32[3,1024,1024]{2,1,0:T(8,128)} fusion(f32[1,1024,1024]{2,1,0:T(8,128)S(1)} %convolution_bitcast_fusion, f32[1,1024,1024]{2,1,0:T(8,128)S(1)} %convolution_bitcast_fusion.1, f32[1,1024,1024]{2,1,0:T(8,128)S(1)} %convolution_bitcast_fusion.2), kind=kLoop, calls=%fused_computation | loop fusion | flops 6291456 | bytes 25165824 | tf_op jit(solution)/shard_map/stack | solution.py:267
  262.1 18.4 %copy.6 = f32[3,1024,1024]{1,0,2:T(4,128)} copy(f32[3,1024,1024]{2,1,0:T(8,128)} %pad_maximum_fusion) | data formatting | bytes 25165824 | tf_op jit(solution)/shard_map/stack | solution.py:267
  280.5 0.0 copy-start.2
  280.5 0.0 all-reduce.3.cloned.1.call-update
  280.5 0.6 copy-done.2
  281.1 0.6 dynamic-slice
  282.3 195.9 %all-reduce.3.cloned.1.call-done = f32[3,1024,1024]{1,0,2:T(4,128)} async-done(((f32[3,1024,1024]{1,0,2:T(4,128)}), f32[3,1024,1024]{1,0,2:T(4,128)}) %all-reduce.3.cloned.1.call-update) | async-done | bytes 12582928
  478.3 1.5 dynamic-slice_multiply_fusion
  479.8 1.3 copy.7
  481.1 0.6 copy.10
Async XLA Ops:
  7.2 471.1 %all-reduce.3.cloned.1.call-start = ((), (), s32[]{:S(2)}) async-start(), calls=%async_computation | async-start | bytes 33554432
  7.2 1.0 copy-start
  8.2 0.7 copy-start.1
  69.1 178.2 %collective-permute-start = (bf16[1024,2048]{1,0:T(8,128)(2,1)S(1)}, bf16[1024,2048]{1,0:T(8,128)(2,1)S(1)}, u32[]{:S(2)}, u32[]{:S(2)}) collective-permute-start(bf16[1024,2048]{1,0:T(8,128)(2,1)S(1)} %get-tuple-element.4), channel_id=1, source_target_pairs={{0,16},{16,32},{32,48},{48,64},{64,80},{80,96},{96,112},{112,0},{1... | collective-permute-start | bytes 12582920 | tf_op jit(solution)/shard_map/ppermute | solution.py:254
  69.8 182.4 %collective-permute-start.1 = (bf16[1024,2048]{1,0:T(8,128)(2,1)S(1)}, bf16[1024,2048]{1,0:T(8,128)(2,1)S(1)}, u32[]{:S(2)}, u32[]{:S(2)}) collective-permute-start(bf16[1024,2048]{1,0:T(8,128)(2,1)S(1)} %get-tuple-element.4), channel_id=1, source_target_pairs={{0,112},{16,0},{32,16},{48,32},{64,48},{80,64},{96,80},{112,96},{1... | collective-permute-start | bytes 12582920 | tf_op jit(solution)/shard_map/ppermute | solution.py:254
  280.5 0.7 copy-start.2
Sparse Core Ops, SparseCore 0:
  280.6 197.6 all-reduce.2

commit v2 on v1

--- a/solution.py
+++ b/solution.py
@@ -9,6 +9,7 @@
 
 K = 32
 ITERS = 128
+GROUP = 16
 MESH = pl.DeviceIdType.MESH
 F32 = jnp.float32
 BF16 = jnp.bfloat16
@@ -51,17 +52,27 @@
     return high, mid, low
 
 
-def chain_kernel(
+def program_kernel(
     samps, probes_n, samples,
-    methyl, atlas, ids, scores, zout, dout,
+    methyl, atlas, ids, scores, out,
     pmsg, prcv, gcol, dmsg, drcv, cmsg, crcv, lmsg, lrcv, resid, smsg, srcv, lsplit,
+    nmsg, nrcv, near, znat, zall, pown, pfar, pin, amsg, ain, bsum, ymsg, yin, final, xmsg, xin,
     psem, prsem, dsem, drsem, csem, crsem, lsem, lrsem, ssem, srsem,
+    nsem, nrsem, msem, mrsem, osem, orsem, zsem, zrsem, ysem, yrsem, xsem, xrsem,
 ):
     me_p = lax.axis_index("probe")
     me_s = lax.axis_index("samp")
-    rows, cols = methyl.shape
-    share = rows // probes_n
+    blocks, share, cols = methyl.shape
+    rows = blocks * share
     width = cols // samps
+    phases = share // GROUP
+    core = lax.rem(me_p, 2)
+    z_at = lax.rem(me_p // 2, 4)
+    y_at = me_p // 8
+    sibling = me_p + 1 - 2 * core
+    partner = me_p + 8 - 16 * y_at
+    ahead = lax.rem(me_s + 1, samps)
+    behind = lax.rem(me_s + samps - 1, samps)
 
     barrier = pltpu.get_barrier_semaphore()
 
@@ -72,8 +83,17 @@
             )
             return carry
         lax.fori_loop(1, peers, body, 0)
+
+    def greet_diagonal(step, carry):
+        other = lax.rem(me_p + step, probes_n)
+        for side in (ahead, behind):
+            pl.semaphore_signal(
+                barrier, inc=1, device_id={"samp": side, "probe": other}, device_id_type=MESH
+            )
+        return carry
+    greet("samp", samps, me_s)
     greet("probe", probes_n, me_p)
-    greet("samp", samps, me_s)
+    lax.fori_loop(1, probes_n, greet_diagonal, 0)
 
     kinds = atlas.shape[0]
     select_t = (lax.broadcasted_iota(jnp.int32, (kinds, kinds), 0) == ids[...]).astype(F32)
@@ -83,16 +103,28 @@
     pad = jnp.zeros((K, 128 - share - K), F32)
 
     def project(step, carry):
-        block = methyl[pl.ds(pl.multiple_of(step * 2 * share, 2 * share), 2 * share), :]
+        block = methyl[pl.ds(2 * step, 2)].reshape(2 * share, cols)
         part = dot(panel, block, ((1,), (1,)))
         pmsg[2 * step] = jnp.concatenate([part[:, :share], gram_part, pad], axis=1)
         pmsg[2 * step + 1] = jnp.concatenate([part[:, share:], gram_part, pad], axis=1)
         return carry
     lax.fori_loop(0, probes_n // 2, project, 0)
 
-    pl.semaphore_wait(barrier, probes_n - 1 + samps - 1)
+    pl.semaphore_wait(barrier, probes_n - 1 + samps - 1 + 2 * (probes_n - 1))
     from_p = lambda peer: pmsg.at[peer]
     exchange_start(from_p, prcv, psem, prsem, "probe", probes_n, me_p)
+
+    def bulk(phase):
+        return copy_to(
+            methyl.at[:, pl.ds(pl.multiple_of(phase * GROUP, GROUP), GROUP), :],
+            zall.at[phases + phase], msem.at[phase], mrsem.at[phase], "samp", ahead,
+        )
+
+    def bulk_start(phase, carry):
+        bulk(phase).start()
+        return carry
+    lax.fori_loop(0, phases, bulk_start, 0)
+
     prcv[me_p] = pmsg[me_p]
     exchange_wait(from_p, prcv, psem, prsem, "probe", probes_n, me_p)
     total = prcv[0]
@@ -138,15 +170,17 @@
     drcv[me_p] = dmsg[...]
     exchange_wait(from_d, drcv, dsem, drsem, "probe", probes_n, me_p)
     design4 = drcv[...].reshape(rows, 4 * K)
-    dout[...] = design4
     design = design4.astype(F32).T[:K].astype(BF16)
+    nmsg[...] = design
+    to_next = copy_to(nmsg, nrcv, nsem, nrsem, "samp", ahead)
+    to_next.start()
 
     wgram_part = dot(design, design, ((1,), (1,)))
     wpad = jnp.concatenate([wgram_part, jnp.zeros((K, 128 - K), F32)], axis=1)
 
     def crossing(step, carry):
-        block = methyl[:, pl.ds(pl.multiple_of(step * width, width), width)]
-        cmsg[step] = jnp.concatenate([dot(design, block), wpad], axis=1)
+        at = pl.ds(pl.multiple_of(step * width, width), width)
+        cmsg[step] = jnp.concatenate([dot(design, methyl[:, :, at].reshape(rows, width)), wpad], axis=1)
         return carry
     lax.fori_loop(0, samps, crossing, 0)
     from_c = lambda peer: cmsg.at[peer]
@@ -178,21 +212,22 @@
     lrcv[me_s] = lmsg[...]
     exchange_wait(from_l, lrcv, lsem, lrsem, "samp", samps, me_s)
 
+    part_blocks = 256 // share
+
     def residue(step, carry):
         high, mid, low = split3(lrcv[step])
         stacked = jnp.concatenate([high, mid, low, jnp.zeros_like(low)], axis=0)
         at = pl.ds(pl.multiple_of(step * width, width), width)
         lsplit[:, at] = stacked
         sums = jnp.zeros((1, width), F32)
-        for r in range(0, rows, 256):
-            res = methyl[r:r + 256, at].astype(F32) - dot(drcv_rows(drcv, r, 256), stacked)
-            resid[r:r + 256, at] = res
+        for b in range(0, blocks, part_blocks):
+            res = methyl[b:b + part_blocks, :, at].reshape(256, width).astype(F32) - dot(
+                drcv[b:b + part_blocks].reshape(256, 4 * K), stacked
+            )
+            resid[b * share:b * share + 256, at] = res
             sums = sums + jnp.sum(res * res, axis=0, keepdims=True)
         smsg[:, at] = sums
         return carry
-
-    def drcv_rows(ref, start, count):
-        return ref[start // share:(start + count) // share].reshape(count, 4 * K)
     lax.fori_loop(0, samps, residue, 0)
     from_s = lambda peer: smsg
     exchange_start(from_s, srcv, ssem, srsem, "samp", samps, me_s)
@@ -205,26 +240,192 @@
 
     def normalize(step, carry):
         at = pl.ds(pl.multiple_of(step * width, width), width)
-        zout[:, at] = (resid[:, at] * smsg[:, at]).astype(BF16)
+        for b in range(0, blocks, part_blocks):
+            value = (resid[b * share:b * share + 256, at] * smsg[:, at]).astype(BF16)
+            value = value.reshape(part_blocks, share, width)
+            znat[b:b + part_blocks, :, at] = value
+            for phase in range(phases):
+                zall[phase, b:b + part_blocks, :, at] = value[:, phase * GROUP:(phase + 1) * GROUP]
         return carry
     lax.fori_loop(0, samps, normalize, 0)
 
-
-def chain(mesh, methyl, atlas, panel_ids):
+    to_next.wait_recv()
+    others = nrcv[...].astype(F32)
+    near[...] = jnp.concatenate([others] * 4, axis=0).T.astype(BF16).reshape(blocks, share, 4 * K)
+
+    unit_rows = blocks * GROUP
+
+    def to_sibling(unit):
+        return copy_to(pfar.at[unit], pin.at[unit], osem.at[unit], orsem.at[unit], "probe", sibling)
+
+    def along_z(unit, step):
+        z_to = lax.rem(z_at + step, 4)
+        return copy_to(
+            amsg.at[unit, z_to], ain.at[unit, step], zsem.at[unit, step], zrsem.at[unit, step],
+            "probe", y_at * 8 + z_to * 2 + core,
+        )
+
+    def to_partner(unit):
+        return copy_to(ymsg.at[unit], yin.at[unit], ysem.at[unit], yrsem.at[unit], "probe", partner)
+
+    def to_behind(phase, other):
+        return pltpu.make_async_remote_copy(
+            src_ref=xmsg.at[phase, other], dst_ref=xin.at[me_p, phase],
+            send_sem=xsem.at[phase, other], recv_sem=xrsem.at[phase, me_p],
+            device_id={"samp": behind, "probe": other}, device_id_type=MESH,
+        )
+
+    def prepare(unit):
+        phase = unit - phases
+        bulk(phase).wait_recv()
+        group = near[:, pl.ds(pl.multiple_of(phase * GROUP, GROUP), GROUP), :].reshape(unit_rows, 4 * K)
+
+        def body(step, carry):
+            at = pl.ds(pl.multiple_of(step * width, width), width)
+            raw = zall[unit, :, :, at].reshape(unit_rows, width).astype(F32)
+            value = (raw - dot(group, lsplit[:, at])) * smsg[:, at]
+            zall[unit, :, :, at] = value.astype(BF16).reshape(blocks, GROUP, width)
+            return carry
+        lax.fori_loop(0, samps, body, 0)
+
+    def multiply(unit):
+        def body(step, carry):
+            at = pl.ds(pl.multiple_of(step * 256, 256), 256)
+            other = znat[pl.ds(step * part_blocks, part_blocks)].reshape(256, cols)
+            part = dot(zall[unit].reshape(unit_rows, cols), other, ((1,), (1,)))
+            part = part.reshape(blocks // 2, 2, GROUP, 256)
+            mine = jnp.where(core == 0, part[:, 0], part[:, 1])
+            far = jnp.where(core == 0, part[:, 1], part[:, 0])
+            pown[unit, :, :, at] = mine
+            pfar[unit, :, :, at] = far.astype(BF16)
+            return carry
+        lax.fori_loop(0, rows // 256, body, 0)
+        to_sibling(unit).start()
+
+    def sum_cores(unit):
+        to_sibling(unit).wait_recv()
+        for z in range(4):
+            for y in range(2):
+                both_cores = pown[unit, 4 * y + z] + pin[unit, 4 * y + z].astype(F32)
+                pown[unit, 4 * y + z] = both_cores
+                amsg[unit, z, y] = both_cores.astype(BF16)
+        for step in range(1, 4):
+            along_z(unit, step).start()
+
+    def sum_z(unit):
+        for step in range(1, 4):
+            along_z(unit, step).wait_recv()
+        for y in range(2):
+            value = pown[unit, 4 * y + z_at]
+            for step in range(1, 4):
+                value = value + ain[unit, step, y].astype(F32)
+            bsum[unit, y] = value
+        ymsg[unit] = bsum[unit, 1 - y_at]
+        to_partner(unit).start()
+
+    def sum_y(unit):
+        to_partner(unit).wait_recv()
+        value = (bsum[unit, y_at] + yin[unit]) * (1.0 / (cols * probes_n))
+        tile = unit // phases
+        phase = unit - tile * phases
+        final[tile, pl.ds(pl.multiple_of(phase * GROUP, GROUP), GROUP)] = value
+
+        @pl.when(tile == 1)
+        def _():
+            for other in range(blocks):
+                xmsg[phase, other] = value[:, other * share:(other + 1) * share]
+
+            def send(other, carry):
+                to_behind(phase, other).start()
+                return carry
+            lax.fori_loop(0, blocks, send, 0)
+
+    units = 2 * phases
+    last = units - 1
+
+    def pipeline(unit, carry):
+        @pl.when(unit >= phases)
+        def _():
+            prepare(unit)
+        multiply(unit)
+
+        @pl.when(unit >= 1)
+        def _():
+            sum_cores(unit - 1)
+
+        @pl.when(unit >= 2)
+        def _():
+            sum_z(unit - 2)
+
+        @pl.when(unit >= 3)
+        def _():
+            sum_y(unit - 3)
+        return carry
+    lax.fori_loop(0, last, pipeline, 0)
+    sum_cores(last - 1)
+
+    def drain(unit, carry):
+        sum_z(unit)
+        sum_y(unit - 1)
+        return carry
+    lax.fori_loop(last - 2, last, drain, 0)
+    sum_y(last - 1)
+    out[0] = final[0].T
+    prepare(last)
+    multiply(last)
+    sum_cores(last)
+    sum_z(last)
+    sum_y(last)
+    out[1] = final[1].T
+
+    def receive(phase, carry):
+        def body(other, inner):
+            pltpu.make_async_remote_copy(
+                src_ref=xmsg.at[phase, other], dst_ref=xin.at[other, phase],
+                send_sem=xsem.at[phase, other], recv_sem=xrsem.at[phase, other],
+                device_id={"samp": ahead, "probe": other}, device_id_type=MESH,
+            ).wait_recv()
+            return inner
+        return lax.fori_loop(0, blocks, body, carry)
+    lax.fori_loop(0, phases, receive, 0)
+    out[2] = xin[...].reshape(rows, share)
+
+    def sent(unit, carry):
+        to_sibling(unit).wait_send()
+        for step in range(1, 4):
+            along_z(unit, step).wait_send()
+        to_partner(unit).wait_send()
+        return carry
+    lax.fori_loop(0, units, sent, 0)
+
+    def sent_out(phase, carry):
+        bulk(phase).wait_send()
+
+        def body(other, inner):
+            to_behind(phase, other).wait_send()
+            return inner
+        return lax.fori_loop(0, blocks, body, carry)
+    lax.fori_loop(0, phases, sent_out, 0)
+    to_next.wait_send()
+
+
+def whole(mesh, methyl, atlas, panel_ids):
     samps, probes_n = mesh.shape["samp"], mesh.shape["probe"]
     rows, cols = methyl.shape
     share, width = rows // probes_n, cols // samps
+    phases = share // GROUP
+    units = 2 * phases
+    per_core = probes_n // 2
     vmem = pl.BlockSpec(memory_space=pltpu.VMEM)
     dma = pltpu.SemaphoreType.DMA
     return pl.pallas_call(
-        functools.partial(chain_kernel, samps, probes_n, rows * samps),
+        functools.partial(program_kernel, samps, probes_n, rows * samps),
         out_shape=(
             jax.ShapeDtypeStruct((K, share), F32),
-            jax.ShapeDtypeStruct((rows, cols), BF16),
-            jax.ShapeDtypeStruct((rows, 4 * K), BF16),
+            jax.ShapeDtypeStruct((3, rows, share), F32),
         ),
         in_specs=[vmem] * 3,
-        out_specs=(vmem,) * 3,
+        out_specs=(vmem,) * 2,
         scratch_shapes=[
             pltpu.VMEM((probes_n, K, 128), F32),
             pltpu.VMEM((probes_n, K, 128), F32),
@@ -239,36 +440,39 @@
             pltpu.VMEM((1, cols), F32),
             pltpu.VMEM((samps, 1, cols), F32),
             pltpu.VMEM((4 * K, cols), BF16),
+            pltpu.VMEM((K, rows), BF16),
+            pltpu.VMEM((K, rows), BF16),
+            pltpu.VMEM((probes_n, share, 4 * K), BF16),
+            pltpu.VMEM((probes_n, share, cols), BF16),
+            pltpu.VMEM((units, probes_n, GROUP, cols), BF16),
+            pltpu.VMEM((units, per_core, GROUP, rows), F32),
+            pltpu.VMEM((units, per_core, GROUP, rows), BF16),
+            pltpu.VMEM((units, per_core, GROUP, rows), BF16),
+            pltpu.VMEM((units, 4, 2, GROUP, rows), BF16),
+            pltpu.VMEM((units, 4, 2, GROUP, rows), BF16),
+            pltpu.VMEM((units, 2, GROUP, rows), F32),
+            pltpu.VMEM((units, GROUP, rows), F32),
+            pltpu.VMEM((units, GROUP, rows), F32),
+            pltpu.VMEM((2, share, rows), F32),
+            pltpu.VMEM((phases, probes_n, GROUP, share), F32),
+            pltpu.VMEM((probes_n, phases, GROUP, share), F32),
             dma((probes_n,)), dma((probes_n,)), dma((probes_n,)), dma((probes_n,)),
             dma((samps,)), dma((samps,)), dma((samps,)), dma((samps,)), dma((samps,)), dma((samps,)),
+            dma, dma, dma((phases,)), dma((phases,)), dma((units,)), dma((units,)),
+            dma((units, 4)), dma((units, 4)), dma((units,)), dma((units,)),
+            dma((phases, probes_n)), dma((phases, probes_n)),
         ],
         compiler_params=pltpu.CompilerParams(
-            collective_id=0, has_side_effects=True, vmem_limit_bytes=48 * 1024 * 1024
+            collective_id=0, has_side_effects=True, vmem_limit_bytes=60 * 1024 * 1024
         ),
-        name="chain",
-    )(methyl, atlas, panel_ids.reshape(1, -1))
-
-
-def shifted(value, axis, by):
-    peers = lax.axis_size(axis)
-    return lax.ppermute(value, axis, [(i, (i + by) % peers) for i in range(peers)])
-
-
-def tile_product(first_block, other_block):
-    return dot(first_block, other_block, ((1,), (1,)))
+        name="whole",
+    )(methyl.reshape(probes_n, share, cols), atlas, panel_ids.reshape(1, -1))
 
 
 def solution(mesh):
     def body(methyl, atlas, panel_ids):
-        probes = methyl.shape[1] * mesh.shape["probe"]
-        scores, zscore, design = chain(mesh, methyl, atlas, panel_ids)
-        before = shifted(zscore, "samp", 1)
-        after = shifted(zscore, "samp", -1)
-        tile_terms = jnp.stack(
-            [tile_product(zscore, zscore), tile_product(zscore, before), tile_product(zscore, after)]
-        )
-        tile_totals = lax.psum_scatter(tile_terms, "probe", scatter_dimension=2, tiled=True)
-        return (tile_totals / probes, scores)
+        scores, relmat = whole(mesh, methyl, atlas, panel_ids)
+        return relmat, scores
 
     return jax.shard_map(
         body,

time: 490 us -> 217 us (0.44)
  waiting for transfers between devices: 365 us -> 0 us
  Pallas kernels: 60.3 us -> 212 us
  local copies, waits for them, and re-layouts: 23.1 us -> 4.06 us
  between operations: 14.7 us -> 0.64 us
  matrix products: 13.9 us -> 0 us
  other arithmetic: 6.69 us -> 0 us
  starting transfers between devices: 5.19 us -> 0 us
    unnamed x2 -> x0, waiting for transfers between devices: 196 us -> none
    ppermute x2 -> x0, waiting for transfers between devices: 169 us -> none  [shifted(): lax.ppermute(value, axis, [(i, (i + by) % peers) for i in range(peers)])]
    pallas_call x1, Pallas kernels: 60.3 us -> 212 us  [whole(): pl.pallas_call(functools.partial(program_kernel, samps, probes_n, rows *...]
    another operation x1 -> x0, local copies, waits for them, and re-layouts: 18.4 us -> none  [body(): jnp.stack([tile_product(zscore, zscore), tile_product(zscore, before), ti...]
    dot_general x3 -> x0, matrix products: 13.9 us -> none  [dot(): return lax.dot_general(a, b, (dims, ((), ())), preferred_element_type=F32)]
    another operation x1 -> x0, other arithmetic: 5.19 us -> none  [body(): jnp.stack([tile_product(zscore, zscore), tile_product(zscore, before), ti...]
    ppermute x2 -> x0, starting transfers between devices: 5.15 us -> none  [shifted(): lax.ppermute(value, axis, [(i, (i + by) % peers) for i in range(peers)])]
  transfers between devices with their start and end apart: 3 -> 0, of which waited for: 3 -> 0; matrix products, arithmetic and copies ran while one was open for 2% -> 0% of each run, Pallas kernels for 0% -> 0%
where the time goes in v2:
time: 217 us
  Pallas kernels  212 us (98%)
  local copies, waits for them, and re-layouts  4.06 us (2%)
    pallas_call x1, Pallas kernels, whole(): pl.pallas_call(functools.partial(program_kernel, samps, probes_n, rows *...  212 us

profile of v2, /device:TPU:1, one launch (start us, length us, event | category | flops | bytes accessed | tf_op | source)
XLA Modules:
  0.0 217.0 jit_solution(16344064911249509437)
XLA Ops:
  0.6 212.3 %whole.1 = (f32[32,64]{1,0:T(8,128)}, f32[3,1024,64]{2,1,0:T(8,128)}) custom-call(bf16[16,64,2048]{2,1,0:T(8,128)(2,1)} %bitcast.2, bf16[64,2048]{1,0:T(8,128)(2,1)} %atlas.1, s32[1,64]{1,0:T(1,128)} %bitcast.3), custom_call_target="tpu_custom_call" | custom-call | tf_op jit(solution)/shard_map/whole/pallas_call | solution.py:421
  212.9 2.7 %copy.5 = f32[3,1024,64]{1,2,0:T(8,128)} copy(f32[3,1024,64]{2,1,0:T(8,128)} %get-tuple-element.6) | data formatting | bytes 1572864
  215.6 1.3 copy.7

commit v3 on v2

--- a/solution.py
+++ b/solution.py
@@ -10,6 +10,13 @@
 K = 32
 ITERS = 128
 GROUP = 16
+PIECE = 4
+BULK = (4, 5, 6, 7, 8)
+RELAY = (0, 1, 2, 3, 4, 5, 6, 7)
+EACH = 2
+EACH_RELAY = 2
+LAG_Z = 2
+LAG_Y = 4
 MESH = pl.DeviceIdType.MESH
 F32 = jnp.float32
 BF16 = jnp.bfloat16
@@ -56,9 +63,9 @@
     samps, probes_n, samples,
     methyl, atlas, ids, scores, out,
     pmsg, prcv, gcol, dmsg, drcv, cmsg, crcv, lmsg, lrcv, resid, smsg, srcv, lsplit,
-    nmsg, nrcv, near, znat, zall, pown, pfar, pin, amsg, ain, bsum, ymsg, yin, final, xmsg, xin,
+    nmsg, nrcv, near, znat, raw, pown, pfar, pin, amsg, ain, bsum, ymsg, yin, final, xmsg, xin,
     psem, prsem, dsem, drsem, csem, crsem, lsem, lrsem, ssem, srsem,
-    nsem, nrsem, msem, mrsem, osem, orsem, zsem, zrsem, ysem, yrsem, xsem, xrsem,
+    nsem, nrsem, msem, mrsem, rsem, rrsem, osem, orsem, zsem, zrsem, ysem, yrsem, xsem, xrsem,
 ):
     me_p = lax.axis_index("probe")
     me_s = lax.axis_index("samp")
@@ -71,8 +78,13 @@
     y_at = me_p // 8
     sibling = me_p + 1 - 2 * core
     partner = me_p + 8 - 16 * y_at
-    ahead = lax.rem(me_s + 1, samps)
-    behind = lax.rem(me_s + samps - 1, samps)
+    odd = lax.rem(me_s, 2)
+    mate = me_s + 1 - 2 * odd
+    cousin = lax.rem(me_s + samps - 1 + 2 * odd, samps)
+    onward = lax.rem(me_s + samps + 2 - 4 * odd, samps)
+    reach = cols // 2
+    held = pl.ds(pl.multiple_of(odd * reach, reach), reach)
+    given = pl.ds(pl.multiple_of((1 - odd) * reach, reach), reach)
 
     barrier = pltpu.get_barrier_semaphore()
 
@@ -84,16 +96,8 @@
             return carry
         lax.fori_loop(1, peers, body, 0)
 
-    def greet_diagonal(step, carry):
-        other = lax.rem(me_p + step, probes_n)
-        for side in (ahead, behind):
-            pl.semaphore_signal(
-                barrier, inc=1, device_id={"samp": side, "probe": other}, device_id_type=MESH
-            )
-        return carry
     greet("samp", samps, me_s)
     greet("probe", probes_n, me_p)
-    lax.fori_loop(1, probes_n, greet_diagonal, 0)
 
     kinds = atlas.shape[0]
     select_t = (lax.broadcasted_iota(jnp.int32, (kinds, kinds), 0) == ids[...]).astype(F32)
@@ -110,20 +114,42 @@
         return carry
     lax.fori_loop(0, probes_n // 2, project, 0)
 
-    pl.semaphore_wait(barrier, probes_n - 1 + samps - 1 + 2 * (probes_n - 1))
+    pl.semaphore_wait(barrier, probes_n - 1 + samps - 1)
     from_p = lambda peer: pmsg.at[peer]
     exchange_start(from_p, prcv, psem, prsem, "probe", probes_n, me_p)
 
-    def bulk(phase):
+    parts = blocks // PIECE
+    pieces = phases * parts
+
+    def place(piece):
+        phase = piece // parts
+        return phase, pl.ds((piece - phase * parts) * PIECE, PIECE)
+
+    def bulk(piece):
+        phase, at = place(piece)
         return copy_to(
-            methyl.at[:, pl.ds(pl.multiple_of(phase * GROUP, GROUP), GROUP), :],
-            zall.at[phases + phase], msem.at[phase], mrsem.at[phase], "samp", ahead,
-        )
-
-    def bulk_start(phase, carry):
-        bulk(phase).start()
-        return carry
-    lax.fori_loop(0, phases, bulk_start, 0)
+            methyl.at[at, pl.ds(pl.multiple_of(phase * GROUP, GROUP), GROUP), given],
+            raw.at[0, phase, at], msem.at[piece], mrsem.at[piece], "samp", mate,
+        )
+
+    def relay(piece):
+        phase, at = place(piece)
+        return copy_to(
+            raw.at[0, phase, at], raw.at[1, phase, at], rsem.at[piece], rrsem.at[piece], "samp", onward,
+        )
+
+    def bulk_start(first, past):
+        def body(piece, carry):
+            bulk(piece).start()
+            return carry
+        lax.fori_loop(first, past, body, 0)
+
+    def relay_start(first, past):
+        def body(piece, carry):
+            bulk(piece).wait_recv()
+            relay(piece).start()
+            return carry
+        lax.fori_loop(first, past, body, 0)
 
     prcv[me_p] = pmsg[me_p]
     exchange_wait(from_p, prcv, psem, prsem, "probe", probes_n, me_p)
@@ -158,7 +184,12 @@
         other = jnp.where(left, acc[half:], acc[:half])
         grad = keep + pltpu.roll(other, share, axis=1) - goal
         return jnp.maximum(state - grad, 0.0)
-    state = lax.fori_loop(0, ITERS, descend, jnp.full((half, 128), 1.0 / K, F32))
+    bulk_start(0, BULK[0])
+    state = jnp.full((half, 128), 1.0 / K, F32)
+    for segment in range(4):
+        state = lax.fori_loop(0, ITERS // 4, descend, state)
+        if segment:
+            relay_start(RELAY[segment - 1], RELAY[segment])
     weights = jnp.concatenate([state[:, :share], state[:, share:]], axis=0)
     scores[...] = weights * float(K)
 
@@ -172,8 +203,11 @@
     design4 = drcv[...].reshape(rows, 4 * K)
     design = design4.astype(F32).T[:K].astype(BF16)
     nmsg[...] = design
-    to_next = copy_to(nmsg, nrcv, nsem, nrsem, "samp", ahead)
-    to_next.start()
+
+    def issue(slot):
+        bulk_start(BULK[slot - 1], BULK[slot])
+        relay_start(RELAY[slot + 2], RELAY[slot + 3])
+    issue(1)
 
     wgram_part = dot(design, design, ((1,), (1,)))
     wpad = jnp.concatenate([wgram_part, jnp.zeros((K, 128 - K), F32)], axis=1)
@@ -187,6 +221,7 @@
     exchange_start(from_c, crcv, csem, crsem, "samp", samps, me_s)
     crcv[me_s] = cmsg[me_s]
     exchange_wait(from_c, crcv, csem, crsem, "samp", samps, me_s)
+    issue(2)
     both = crcv[0]
     for peer in range(1, samps):
         both = both + crcv[peer]
@@ -212,6 +247,7 @@
     lrcv[me_s] = lmsg[...]
     exchange_wait(from_l, lrcv, lsem, lrsem, "samp", samps, me_s)
 
+    issue(3)
     part_blocks = 256 // share
 
     def residue(step, carry):
@@ -233,6 +269,11 @@
     exchange_start(from_s, srcv, ssem, srsem, "samp", samps, me_s)
     srcv[me_s] = smsg[...]
     exchange_wait(from_s, srcv, ssem, srsem, "samp", samps, me_s)
+    to_mate = copy_to(nmsg, nrcv.at[0], nsem.at[0], nrsem.at[0], "samp", mate)
+    to_cousin = copy_to(nmsg, nrcv.at[1], nsem.at[1], nrsem.at[1], "samp", cousin)
+    to_mate.start()
+    to_cousin.start()
+    issue(4)
     spread = srcv[0]
     for peer in range(1, samps):
         spread = spread + srcv[peer]
@@ -244,14 +285,13 @@
             value = (resid[b * share:b * share + 256, at] * smsg[:, at]).astype(BF16)
             value = value.reshape(part_blocks, share, width)
             znat[b:b + part_blocks, :, at] = value
-            for phase in range(phases):
-                zall[phase, b:b + part_blocks, :, at] = value[:, phase * GROUP:(phase + 1) * GROUP]
         return carry
     lax.fori_loop(0, samps, normalize, 0)
 
-    to_next.wait_recv()
-    others = nrcv[...].astype(F32)
-    near[...] = jnp.concatenate([others] * 4, axis=0).T.astype(BF16).reshape(blocks, share, 4 * K)
+    def widen(which, copy):
+        copy.wait_recv()
+        others = nrcv[which].astype(F32)
+        near[which] = jnp.concatenate([others] * 4, axis=0).T.astype(BF16).reshape(blocks, share, 4 * K)
 
     unit_rows = blocks * GROUP
 
@@ -268,38 +308,67 @@
     def to_partner(unit):
         return copy_to(ymsg.at[unit], yin.at[unit], ysem.at[unit], yrsem.at[unit], "probe", partner)
 
-    def to_behind(phase, other):
+    def across(which, phase, other, slot):
         return pltpu.make_async_remote_copy(
-            src_ref=xmsg.at[phase, other], dst_ref=xin.at[me_p, phase],
-            send_sem=xsem.at[phase, other], recv_sem=xrsem.at[phase, me_p],
-            device_id={"samp": behind, "probe": other}, device_id_type=MESH,
+            src_ref=xmsg.at[which, phase, other], dst_ref=xin.at[which, slot, phase],
+            send_sem=xsem.at[which, phase, other], recv_sem=xrsem.at[which, phase, slot],
+            device_id={"samp": jnp.where(which == 0, mate, cousin), "probe": other}, device_id_type=MESH,
         )
 
     def prepare(unit):
-        phase = unit - phases
-        bulk(phase).wait_recv()
-        group = near[:, pl.ds(pl.multiple_of(phase * GROUP, GROUP), GROUP), :].reshape(unit_rows, 4 * K)
+        which = unit // phases - 1
+        phase = lax.rem(unit, phases)
+        first, past = phase * parts, (phase + 1) * parts
+
+        @pl.when(which == 1)
+        def _():
+            def arrive(piece, carry):
+                relay(piece).wait_recv()
+                return carry
+            lax.fori_loop(first, past, arrive, 0)
+
+        @pl.when(which == 0)
+        def _():
+            def depart(piece, carry):
+                relay(piece).wait_send()
+                return carry
+            lax.fori_loop(first, past, depart, 0)
+        group = near[which, :, pl.ds(pl.multiple_of(phase * GROUP, GROUP), GROUP), :].reshape(unit_rows, 4 * K)
 
         def body(step, carry):
             at = pl.ds(pl.multiple_of(step * width, width), width)
-            raw = zall[unit, :, :, at].reshape(unit_rows, width).astype(F32)
-            value = (raw - dot(group, lsplit[:, at])) * smsg[:, at]
-            zall[unit, :, :, at] = value.astype(BF16).reshape(blocks, GROUP, width)
+            there = pl.ds(pl.multiple_of(odd * reach + step * width, width), width)
+            value = raw[which, phase, :, :, at].reshape(unit_rows, width).astype(F32)
+            value = (value - dot(group, lsplit[:, there])) * smsg[:, there]
+            raw[which, phase, :, :, at] = value.astype(BF16).reshape(blocks, GROUP, width)
             return carry
-        lax.fori_loop(0, samps, body, 0)
+        lax.fori_loop(0, reach // width, body, 0)
+
+    def put(unit, at, part):
+        part = part.reshape(blocks // 2, 2, GROUP, 256)
+        pown[unit, :, :, at] = jnp.where(core == 0, part[:, 0], part[:, 1])
+        pfar[unit, :, :, at] = jnp.where(core == 0, part[:, 1], part[:, 0]).astype(BF16)
 
     def multiply(unit):
-        def body(step, carry):
-            at = pl.ds(pl.multiple_of(step * 256, 256), 256)
-            other = znat[pl.ds(step * part_blocks, part_blocks)].reshape(256, cols)
-            part = dot(zall[unit].reshape(unit_rows, cols), other, ((1,), (1,)))
-            part = part.reshape(blocks // 2, 2, GROUP, 256)
-            mine = jnp.where(core == 0, part[:, 0], part[:, 1])
-            far = jnp.where(core == 0, part[:, 1], part[:, 0])
-            pown[unit, :, :, at] = mine
-            pfar[unit, :, :, at] = far.astype(BF16)
-            return carry
-        lax.fori_loop(0, rows // 256, body, 0)
+        phase = lax.rem(unit, phases)
+
+        @pl.when(unit < phases)
+        def _():
+            def body(step, carry):
+                group = znat[:, pl.ds(pl.multiple_of(phase * GROUP, GROUP), GROUP), :].reshape(unit_rows, cols)
+                other = znat[pl.ds(step * part_blocks, part_blocks)].reshape(256, cols)
+                put(unit, pl.ds(pl.multiple_of(step * 256, 256), 256), dot(group, other, ((1,), (1,))))
+                return carry
+            lax.fori_loop(0, rows // 256, body, 0)
+
+        @pl.when(unit >= phases)
+        def _():
+            def body(step, carry):
+                group = raw[unit // phases - 1, phase].reshape(unit_rows, reach)
+                other = znat[pl.ds(step * part_blocks, part_blocks), :, held].reshape(256, reach)
+                put(unit, pl.ds(pl.multiple_of(step * 256, 256), 256), dot(group, other, ((1,), (1,))))
+                return carry
+            lax.fori_loop(0, rows // 256, body, 0)
         to_sibling(unit).start()
 
     def sum_cores(unit):
@@ -330,65 +399,67 @@
         phase = unit - tile * phases
         final[tile, pl.ds(pl.multiple_of(phase * GROUP, GROUP), GROUP)] = value
 
-        @pl.when(tile == 1)
+        @pl.when(tile >= 1)
         def _():
             for other in range(blocks):
-                xmsg[phase, other] = value[:, other * share:(other + 1) * share]
+                xmsg[tile - 1, phase, other] = value[:, other * share:(other + 1) * share]
 
             def send(other, carry):
-                to_behind(phase, other).start()
+                across(tile - 1, phase, other, me_p).start()
                 return carry
             lax.fori_loop(0, blocks, send, 0)
 
-    units = 2 * phases
-    last = units - 1
+    units = 3 * phases
 
     def pipeline(unit, carry):
-        @pl.when(unit >= phases)
+        bulk_start(
+            jnp.minimum(BULK[4] + unit * EACH, pieces), jnp.minimum(BULK[4] + unit * EACH + EACH, pieces)
+        )
+
+        @pl.when(unit == phases)
+        def _():
+            widen(0, to_mate)
+
+        @pl.when(unit == 2 * phases)
+        def _():
+            widen(1, to_cousin)
+
+        @pl.when(jnp.logical_and(unit >= phases, unit < units))
         def _():
             prepare(unit)
-        multiply(unit)
-
-        @pl.when(unit >= 1)
+
+        @pl.when(unit < units)
+        def _():
+            multiply(unit)
+
+        @pl.when(jnp.logical_and(unit >= 1, unit < units + 1))
         def _():
             sum_cores(unit - 1)
 
-        @pl.when(unit >= 2)
-        def _():
-            sum_z(unit - 2)
-
-        @pl.when(unit >= 3)
-        def _():
-            sum_y(unit - 3)
-        return carry
-    lax.fori_loop(0, last, pipeline, 0)
-    sum_cores(last - 1)
-
-    def drain(unit, carry):
-        sum_z(unit)
-        sum_y(unit - 1)
-        return carry
-    lax.fori_loop(last - 2, last, drain, 0)
-    sum_y(last - 1)
-    out[0] = final[0].T
-    prepare(last)
-    multiply(last)
-    sum_cores(last)
-    sum_z(last)
-    sum_y(last)
-    out[1] = final[1].T
+        @pl.when(jnp.logical_and(unit >= LAG_Z, unit < units + LAG_Z))
+        def _():
+            sum_z(unit - LAG_Z)
+
+        @pl.when(unit >= LAG_Y)
+        def _():
+            sum_y(unit - LAG_Y)
+        relay_start(
+            jnp.minimum(RELAY[7] + unit * EACH_RELAY, pieces),
+            jnp.minimum(RELAY[7] + unit * EACH_RELAY + EACH_RELAY, pieces),
+        )
+        return carry
+    lax.fori_loop(0, units + LAG_Y, pipeline, 0)
+    out[0] = final[0]
 
     def receive(phase, carry):
         def body(other, inner):
-            pltpu.make_async_remote_copy(
-                src_ref=xmsg.at[phase, other], dst_ref=xin.at[other, phase],
-                send_sem=xsem.at[phase, other], recv_sem=xrsem.at[phase, other],
-                device_id={"samp": ahead, "probe": other}, device_id_type=MESH,
-            ).wait_recv()
+            across(0, phase, other, other).wait_recv()
+            across(1, phase, other, other).wait_recv()
             return inner
         return lax.fori_loop(0, blocks, body, carry)
     lax.fori_loop(0, phases, receive, 0)
-    out[2] = xin[...].reshape(rows, share)
+    out[2 - odd] = final[1] + xin[0].reshape(rows, share).T
+    out[1 + odd] = final[2] + xin[1].reshape(rows, share).T
 
     def sent(unit, carry):
         to_sibling(unit).wait_send()
@@ -399,14 +470,19 @@
     lax.fori_loop(0, units, sent, 0)
 
     def sent_out(phase, carry):
-        bulk(phase).wait_send()
+        def leave(piece, inner):
+            bulk(piece).wait_send()
+            return inner
+        lax.fori_loop(phase * parts, (phase + 1) * parts, leave, 0)
 
         def body(other, inner):
-            to_behind(phase, other).wait_send()
+            across(0, phase, other, me_p).wait_send()
+            across(1, phase, other, me_p).wait_send()
             return inner
         return lax.fori_loop(0, blocks, body, carry)
     lax.fori_loop(0, phases, sent_out, 0)
-    to_next.wait_send()
+    to_mate.wait_send()
+    to_cousin.wait_send()
 
 
 def whole(mesh, methyl, atlas, panel_ids):
@@ -414,7 +490,8 @@
     rows, cols = methyl.shape
     share, width = rows // probes_n, cols // samps
     phases = share // GROUP
-    units = 2 * phases
+    units = 3 * phases
+    pieces = phases * (probes_n // PIECE)
     per_core = probes_n // 2
     vmem = pl.BlockSpec(memory_space=pltpu.VMEM)
     dma = pltpu.SemaphoreType.DMA
@@ -422,7 +499,7 @@
         functools.partial(program_kernel, samps, probes_n, rows * samps),
         out_shape=(
             jax.ShapeDtypeStruct((K, share), F32),
-            jax.ShapeDtypeStruct((3, rows, share), F32),
+            jax.ShapeDtypeStruct((3, share, rows), F32),
         ),
         in_specs=[vmem] * 3,
         out_specs=(vmem,) * 2,
@@ -441,10 +518,10 @@
             pltpu.VMEM((samps, 1, cols), F32),
             pltpu.VMEM((4 * K, cols), BF16),
             pltpu.VMEM((K, rows), BF16),
-            pltpu.VMEM((K, rows), BF16),
-            pltpu.VMEM((probes_n, share, 4 * K), BF16),
+            pltpu.VMEM((2, K, rows), BF16),
+            pltpu.VMEM((2, probes_n, share, 4 * K), BF16),
             pltpu.VMEM((probes_n, share, cols), BF16),
-            pltpu.VMEM((units, probes_n, GROUP, cols), BF16),
+            pltpu.VMEM((2, phases, probes_n, GROUP, cols // 2), BF16),
             pltpu.VMEM((units, per_core, GROUP, rows), F32),
             pltpu.VMEM((units, per_core, GROUP, rows), BF16),
             pltpu.VMEM((units, per_core, GROUP, rows), BF16),
@@ -453,14 +530,14 @@
             pltpu.VMEM((units, 2, GROUP, rows), F32),
             pltpu.VMEM((units, GROUP, rows), F32),
             pltpu.VMEM((units, GROUP, rows), F32),
-            pltpu.VMEM((2, share, rows), F32),
-            pltpu.VMEM((phases, probes_n, GROUP, share), F32),
-            pltpu.VMEM((probes_n, phases, GROUP, share), F32),
+            pltpu.VMEM((3, share, rows), F32),
+            pltpu.VMEM((2, phases, probes_n, GROUP, share), F32),
+            pltpu.VMEM((2, probes_n, phases, GROUP, share), F32),
             dma((probes_n,)), dma((probes_n,)), dma((probes_n,)), dma((probes_n,)),
             dma((samps,)), dma((samps,)), dma((samps,)), dma((samps,)), dma((samps,)), dma((samps,)),
-            dma, dma, dma((phases,)), dma((phases,)), dma((units,)), dma((units,)),
+            dma((2,)), dma((2,)), dma((pieces,)), dma((pieces,)), dma((pieces,)), dma((pieces,)), dma((units,)), dma((units,)),
             dma((units, 4)), dma((units, 4)), dma((units,)), dma((units,)),
-            dma((phases, probes_n)), dma((phases, probes_n)),
+            dma((2, phases, probes_n)), dma((2, phases, probes_n)),
         ],
         compiler_params=pltpu.CompilerParams(
             collective_id=0, has_side_effects=True, vmem_limit_bytes=60 * 1024 * 1024
@@ -472,7 +549,7 @@
 def solution(mesh):
     def body(methyl, atlas, panel_ids):
         scores, relmat = whole(mesh, methyl, atlas, panel_ids)
-        return relmat, scores
+        return jnp.swapaxes(relmat, 1, 2), scores
 
     return jax.shard_map(
         body,

time: 217 us -> 155 us (0.71)
  Pallas kernels: 212 us -> 150 us
    pallas_call x1, Pallas kernels: 212 us -> 150 us  [whole(): pl.pallas_call(functools.partial(program_kernel, samps, probes_n, rows *...]
where the time goes in v3:
time: 155 us; the launch traced here: 154 us
  Pallas kernels  150 us (97%)
  local copies, waits for them, and re-layouts  3.41 us (2%)
    pallas_call x1, Pallas kernels, whole(): pl.pallas_call(functools.partial(program_kernel, samps, probes_n, rows *...  150 us
    unnamed x2, local copies, waits for them, and re-layouts  3.41 us

profile of v3, /device:TPU:1, one launch (start us, length us, event | category | flops | bytes accessed | tf_op | source)
XLA Modules:
  0.0 154.4 jit_solution(12398424063654046396)
XLA Ops:
  0.6 150.4 %whole.1 = (f32[32,64]{1,0:T(8,128)}, f32[3,64,1024]{2,1,0:T(8,128)}) custom-call(bf16[16,64,2048]{2,1,0:T(8,128)(2,1)} %bitcast.3, bf16[64,2048]{1,0:T(8,128)(2,1)} %atlas.1, s32[1,64]{1,0:T(1,128)} %bitcast.5), custom_call_target="tpu_custom_call" | custom-call | tf_op jit(solution)/shard_map/whole/pallas_call | solution.py:498
  151.0 2.1 %copy.7 = f32[3,1024,64]{1,2,0:T(8,128)} copy(f32[3,1024,64]{1,2,0:T(8,128)} %bitcast.4) | data formatting | bytes 1572864
  153.1 1.3 copy.8

commit v4 on v3

v4 whole, which is shorter than its diff:
```python
import functools

import jax
import jax.numpy as jnp
from jax import lax
from jax.experimental import pallas as pl
from jax.experimental.pallas import tpu as pltpu
from jax.sharding import PartitionSpec as P

K = 32
ITERS = 128
GROUP = 16
PIECE = 4
BULK = (3, 4, 5, 6, 8)
RELAY = (0, 0, 0, 1, 2, 3, 4, 5)
EACH = 2
PACE = 2
LAGS = (1, 3, 5, 7, 9)
ORDER = (0, 1, 2, 4, 3, 5, 6, 7, 8, 9, 10, 11)
MESH = pl.DeviceIdType.MESH
F32 = jnp.float32
BF16 = jnp.bfloat16


def dot(a, b, dims=((1,), (0,))):
    return lax.dot_general(a, b, (dims, ((), ())), preferred_element_type=F32)


def copy_to(src, dst, send_sem, recv_sem, axis, peer):
    return pltpu.make_async_remote_copy(
        src_ref=src, dst_ref=dst, send_sem=send_sem, recv_sem=recv_sem,
        device_id={axis: peer}, device_id_type=MESH,
    )


def exchange_start(src_of, dst, send_sem, recv_sem, axis, peers, me):
    def body(step, carry):
        peer = lax.rem(me + step, peers)
        copy_to(src_of(peer), dst.at[me], send_sem, recv_sem, axis, peer).start()
        return carry
    lax.fori_loop(1, peers, body, 0)


def exchange_wait(dst, send_sem, recv_sem, axis, peers, me):
    rest = dst.at[pl.ds(0, peers - 1)]
    copy = copy_to(rest, rest, send_sem, recv_sem, axis, lax.rem(me + 1, peers))
    copy.wait_recv()
    copy.wait_send()


def split3(value):
    high = value.astype(BF16)
    rest = value - high.astype(F32)
    mid = rest.astype(BF16)
    low = (rest - mid.astype(F32)).astype(BF16)
    return high, mid, low


def program_kernel(
    samps, probes_n, samples,
    methyl, atlas, ids, scores, out,
    pmsg, prcv, gcol, dmsg, drcv, cmsg, crcv, lmsg, lrcv, resid, smsg, srcv, lsplit,
    nmsg, nrcv, near, znat, raw, pown, pfar, pin, amsg, ain, fmsg, fin, bsum, ymsg, yin, final, xin, sin,
    psem, prsem, dsem, drsem, csem, crsem, lsem, lrsem, ssem, srsem,
    nsem, nrsem, msem, mrsem, rsem, rrsem, osem, orsem, zsem, zrsem, fsem, frsem, ysem, yrsem, xsem, xrsem, wsem, wrsem,
):
    me_p = lax.axis_index("probe")
    me_s = lax.axis_index("samp")
    blocks, share, cols = methyl.shape
    rows = blocks * share
    width = cols // samps
    phases = share // GROUP
    core = lax.rem(me_p, 2)
    z_at = lax.rem(me_p // 2, 4)
    y_at = me_p // 8
    sibling = me_p + 1 - 2 * core
    partner = me_p + 8 - 16 * y_at
    odd = lax.rem(me_s, 2)
    mate = me_s + 1 - 2 * odd
    cousin = lax.rem(me_s + samps - 1 + 2 * odd, samps)
    onward = lax.rem(me_s + samps + 2 - 4 * odd, samps)
    reach = cols // 2
    held = pl.ds(pl.multiple_of(odd * reach, reach), reach)
    given = pl.ds(pl.multiple_of((1 - odd) * reach, reach), reach)

    barrier = pltpu.get_barrier_semaphore()

    def greet(axis, peers, me):
        def body(step, carry):
            pl.semaphore_signal(
                barrier, inc=1, device_id={axis: lax.rem(me + step, peers)}, device_id_type=MESH
            )
            return carry
        lax.fori_loop(1, peers, body, 0)

    greet("samp", samps, me_s)
    greet("probe", probes_n, me_p)

    kinds = atlas.shape[0]
    select_t = (lax.broadcasted_iota(jnp.int32, (kinds, kinds), 0) == ids[...]).astype(F32)
    selector = select_t.T[:K].astype(BF16)
    panel = dot(selector, atlas[...]).astype(BF16)
    gram_part = dot(panel, panel, ((1,), (1,)))
    pad = jnp.zeros((K, 128 - share - K), F32)

    def project(step, carry):
        block = methyl[pl.ds(2 * step, 2)].reshape(2 * share, cols)
        part = dot(panel, block, ((1,), (1,)))
        pmsg[2 * step] = jnp.concatenate([part[:, :share], gram_part, pad], axis=1)
        pmsg[2 * step + 1] = jnp.concatenate([part[:, share:], gram_part, pad], axis=1)
        return carry
    lax.fori_loop(0, probes_n // 2, project, 0)

    pl.semaphore_wait(barrier, probes_n - 1 + samps - 1)
    from_p = lambda peer: pmsg.at[peer]
    exchange_start(from_p, prcv, psem, prsem, "probe", probes_n, me_p)

    parts = blocks // PIECE
    pieces = phases * parts

    def place(piece):
        phase = piece // parts
        return phase, pl.ds((piece - phase * parts) * PIECE, PIECE)

    def bulk(piece):
        phase, at = place(piece)
        return copy_to(
            methyl.at[at, pl.ds(pl.multiple_of(phase * GROUP, GROUP), GROUP), given],
            raw.at[0, phase, at], msem, mrsem.at[piece], "samp", mate,
        )

    def relay(piece):
        phase, at = place(piece)
        return copy_to(
            raw.at[0, phase, at], raw.at[1, phase, at], rsem.at[piece], rrsem.at[piece], "samp", onward,
        )

    def bulk_start(first, past):
        def body(piece, carry):
            bulk(piece).start()
            return carry
        lax.fori_loop(first, past, body, 0)

    def relay_start(first, past):
        def body(piece, carry):
            bulk(piece).wait_recv()
            relay(piece).start()
            return carry
        lax.fori_loop(first, past, body, 0)

    prcv[me_p] = pmsg[me_p]
    exchange_wait(prcv, psem, prsem, "probe", probes_n, me_p)
    total = prcv[0]
    for peer in range(1, probes_n):
        total = total + prcv[peer]
    gram = total[:, share:share + K]

    diag = lax.broadcasted_iota(jnp.int32, (K, K), 0) == lax.broadcasted_iota(jnp.int32, (K, K), 1)
    trace = jnp.sum(jnp.where(diag, gram, 0.0), axis=(0, 1), keepdims=True)
    rate = 1.0 / trace
    moving = jnp.where(diag, 1.0, 0.0) - gram * rate
    for k in range(K):
        gcol[k] = jnp.broadcast_to(moving[:, k:k + 1], (K, 128))
    goal = total * rate

    def descend(step, state):
        sums = [goal, None]
        for k in range(K):
            term = gcol[k] * jnp.broadcast_to(state[k:k + 1, :], (K, 128))
            sums[k % 2] = term if sums[k % 2] is None else sums[k % 2] + term
        return jnp.maximum(sums[0] + sums[1], 0.0)
    bulk_start(0, BULK[0])
    state = jnp.full((K, 128), 1.0 / K, F32)
    for segment in range(4):
        state = lax.fori_loop(0, ITERS // 4, descend, state)
        if segment:
            relay_start(RELAY[segment - 1], RELAY[segment])
    weights = state[:, :share]
    scores[...] = weights * float(K)

    four = jnp.concatenate([weights] * 4, axis=0)
    wide = jnp.concatenate([four, jnp.zeros((4 * K, 128 - share), F32)], axis=1)
    dmsg[...] = wide.T[:share].astype(BF16)
    from_d = lambda peer: dmsg
    exchange_start(from_d, drcv, dsem, drsem, "probe", probes_n, me_p)
    drcv[me_p] = dmsg[...]
    exchange_wait(drcv, dsem, drsem, "probe", probes_n, me_p)
    design4 = drcv[...].reshape(rows, 4 * K)
    design = design4.astype(F32).T[:K].astype(BF16)
    nmsg[...] = design

    def issue(slot):
        bulk_start(BULK[slot - 1], BULK[slot])
        relay_start(RELAY[slot + 2], RELAY[slot + 3])
    issue(1)

    wgram_part = dot(design, design, ((1,), (1,)))
    wpad = jnp.concatenate([wgram_part, jnp.zeros((K, 128 - K), F32)], axis=1)

    def crossing(step, carry):
        at = pl.ds(pl.multiple_of(step * width, width), width)
        cmsg[step] = jnp.concatenate([dot(design, methyl[:, :, at].reshape(rows, width)), wpad], axis=1)
        return carry
    lax.fori_loop(0, samps, crossing, 0)
    from_c = lambda peer: cmsg.at[peer]
    exchange_start(from_c, crcv, csem, crsem, "samp", samps, me_s)
    crcv[me_s] = cmsg[me_s]
    exchange_wait(crcv, csem, crsem, "samp", samps, me_s)
    issue(2)
    both = crcv[0]
    for peer in range(1, samps):
        both = both + crcv[peer]

    matrix = both[:, width:]
    row_id = lax.broadcasted_iota(jnp.int32, (K, 128), 0)
    lane_id = lax.broadcasted_iota(jnp.int32, (K, 128), 1)
    matrix = matrix + jnp.where(row_id == lane_id, 0.0001 * samples, 0.0)
    right = both[:, :width]
    row_w = lax.broadcasted_iota(jnp.int32, (K, 1), 0)
    for k in range(K):
        column = matrix[:, k:k + 1]
        pivot = 1.0 / matrix[k:k + 1, k:k + 1]
        factor = jnp.where(row_w == k, 0.0, column * pivot)
        matrix_row = matrix[k:k + 1, :]
        right_row = right[k:k + 1, :]
        matrix = matrix - factor * matrix_row
        right = right - factor * right_row
    pivots = jnp.sum(jnp.where(row_id == lane_id, matrix, 0.0), axis=1, keepdims=True)
    lmsg[...] = right / pivots
    from_l = lambda peer: lmsg
    exchange_start(from_l, lrcv, lsem, lrsem, "samp", samps, me_s)
    lrcv[me_s] = lmsg[...]
    exchange_wait(lrcv, lsem, lrsem, "samp", samps, me_s)

    issue(3)
    part_blocks = 256 // share

    def residue(step, carry):
        high, mid, low = split3(lrcv[step])
        stacked = jnp.concatenate([high, mid, low, jnp.zeros_like(low)], axis=0)
        at = pl.ds(pl.multiple_of(step * width, width), width)
        lsplit[:, at] = stacked
        sums = jnp.zeros((1, width), F32)
        for b in range(0, blocks, part_blocks):
            res = methyl[b:b + part_blocks, :, at].reshape(256, width).astype(F32) - dot(
                drcv[b:b + part_blocks].reshape(256, 4 * K), stacked
            )
            resid[b * share:b * share + 256, at] = res
            sums = sums + jnp.sum(res * res, axis=0, keepdims=True)
        smsg[:, at] = sums
        return carry
    lax.fori_loop(0, samps, residue, 0)
    from_s = lambda peer: smsg
    exchange_start(from_s, srcv, ssem, srsem, "samp", samps, me_s)
    srcv[me_s] = smsg[...]
    exchange_wait(srcv, ssem, srsem, "samp", samps, me_s)
    to_mate = copy_to(nmsg, nrcv.at[0], nsem.at[0], nrsem.at[0], "samp", mate)
    to_cousin = copy_to(nmsg, nrcv.at[1], nsem.at[1], nrsem.at[1], "samp", cousin)
    to_mate.start()
    to_cousin.start()
    issue(4)
    spread = srcv[0]
    for peer in range(1, samps):
        spread = spread + srcv[peer]
    smsg[...] = lax.rsqrt(spread * (1.0 / samples) + 1e-06)

    def normalize(step, carry):
        at = pl.ds(pl.multiple_of(step * width, width), width)
        for b in range(0, blocks, part_blocks):
            value = (resid[b * share:b * share + 256, at] * smsg[:, at]).astype(BF16)
            value = value.reshape(part_blocks, share, width)
            znat[b:b + part_blocks, :, at] = value
        return carry
    lax.fori_loop(0, samps, normalize, 0)

    def widen(which, copy):
        copy.wait_recv()
        others = nrcv[which].astype(F32)
        near[which] = jnp.concatenate([others] * 4, axis=0).T.astype(BF16).reshape(blocks, share, 4 * K)

    unit_rows = blocks * GROUP

    def to_sibling(unit):
        return copy_to(pfar.at[unit], pin.at[unit], osem, orsem.at[unit], "probe", sibling)

    def along_z(unit, way):
        z_to = lax.rem(z_at + 1 + 2 * way, 4)
        return copy_to(
            amsg.at[unit, way], ain.at[unit, way], zsem, zrsem.at[unit],
            "probe", y_at * 8 + z_to * 2 + core,
        )

    def far_z(unit, way):
        z_to = lax.rem(z_at + 1 + 2 * way, 4)
        return copy_to(
            fmsg.at[unit, way], fin.at[unit, way], fsem, frsem.at[unit],
            "probe", y_at * 8 + z_to * 2 + core,
        )

    def to_partner(unit):
        return copy_to(ymsg.at[unit], yin.at[unit], ysem, yrsem.at[unit], "probe", partner)

    pair = 2 * GROUP
    mine = me_p // 2

    def across(which, part, chip):
        return pltpu.make_async_remote_copy(
            src_ref=final.at[1 + which, pl.ds(part * pair, pair), pl.ds(pl.multiple_of(chip * 128, 128), 128)],
            dst_ref=xin.at[which, part, mine],
            send_sem=xsem, recv_sem=xrsem.at[which, part],
            device_id={"samp": (mate, cousin)[which], "probe": 2 * chip + core}, device_id_type=MESH,
        )

    def swap(which, part):
        return copy_to(xin.at[which, part], sin.at[which, part], wsem, wrsem.at[which, part], "probe", sibling)

    def arrived(src, dst, send_sem, recv_sem):
        return copy_to(src, dst, send_sem, recv_sem, "probe", sibling)

    def prepare(unit):
        which, phase = unit // phases - 1, unit % phases
        for piece in range(phase * parts, (phase + 1) * parts):
            if which:
                relay(piece).wait_recv()
            else:
                relay(piece).wait_send()
        group = near[which, :, pl.ds(pl.multiple_of(phase * GROUP, GROUP), GROUP), :].reshape(unit_rows, 4 * K)

        def body(step, carry):
            at = pl.ds(pl.multiple_of(step * width, width), width)
            there = pl.ds(pl.multiple_of(odd * reach + step * width, width), width)
            value = raw[which, phase, :, :, at].reshape(unit_rows, width).astype(F32)
            value = (value - dot(group, lsplit[:, there])) * smsg[:, there]
            raw[which, phase, :, :, at] = value.astype(BF16).reshape(blocks, GROUP, width)
            return carry
        lax.fori_loop(0, reach // width, body, 0)

    def put(unit, at, part):
        part = part.reshape(blocks // 2, 2, GROUP, 256)
        pown[unit, :, :, at] = jnp.where(core == 0, part[:, 0], part[:, 1])
        pfar[unit, :, :, at] = jnp.where(core == 0, part[:, 1], part[:, 0]).astype(BF16)

    def multiply(unit):
        which, phase = unit // phases - 1, unit % phases

        def body(step, carry):
            theirs = pl.ds(step * part_blocks, part_blocks)
            if unit < phases:
                group = znat[:, phase * GROUP:(phase + 1) * GROUP, :].reshape(unit_rows, cols)
                other = znat[theirs].reshape(256, cols)
            else:
                group = raw[which, phase].reshape(unit_rows, reach)
                other = znat[theirs, :, held].reshape(256, reach)
            put(unit, pl.ds(pl.multiple_of(step * 256, 256), 256), dot(group, other, ((1,), (1,))))
            return carry
        lax.fori_loop(0, rows // 256, body, 0)
        to_sibling(unit).start()

    def sum_cores(unit):
        to_sibling(unit).wait_recv()
        for block in range(blocks // 2):
            pown[unit, block] = pown[unit, block] + pin[unit, block].astype(F32)
        across_z = lax.rem(z_at + 2, 4)
        for way in range(2):
            fmsg[unit, way] = pown[unit, 4 * way + across_z].astype(BF16)
            far_z(unit, way).start()

    def sum_far(unit):
        arrived(fmsg.at[unit], fin.at[unit], fsem, frsem.at[unit]).wait_recv()
        for way in range(2):
            z_to = lax.rem(z_at + 1 + 2 * way, 4)
            amsg[unit, way, way] = (pown[unit, 4 * way + z_to] + fin[unit, way].astype(F32)).astype(BF16)
            amsg[unit, way, 1 - way] = pown[unit, 4 * (1 - way) + z_to].astype(BF16)
            along_z(unit, way).start()

    def sum_z(unit):
        arrived(amsg.at[unit], ain.at[unit], zsem, zrsem.at[unit]).wait_recv()
        for y in range(2):
            bsum[unit, y] = (
                pown[unit, 4 * y + z_at] + ain[unit, 0, y].astype(F32) + ain[unit, 1, y].astype(F32)
            )
        ymsg[unit] = bsum[unit, 1 - y_at].astype(BF16)
        to_partner(unit).start()

    def sum_y(unit):
        to_partner(unit).wait_recv()
        value = (bsum[unit, y_at] + yin[unit].astype(F32)) * (1.0 / (cols * probes_n))
        tile, phase = divmod(unit, phases)
        final[tile, phase * GROUP:(phase + 1) * GROUP] = value
        if tile and phase % 2:
            def send(step, carry):
                across(tile - 1, phase // 2, lax.rem(mine + step, blocks // 2)).start()
                return carry
            lax.fori_loop(0, blocks // 2, send, 0)

    def pass_on(unit):
        tile, phase = divmod(unit, phases)
        if tile and phase % 2:
            which, part = tile - 1, phase // 2
            arrived(xin.at[which, part], xin.at[which, part], xsem, xrsem.at[which, part]).wait_recv()
            swap(which, part).start()

    units = 3 * phases

    bulk_done, relay_done = BULK[4], RELAY[7]
    for turn in range(units + LAGS[4]):
        more = min(bulk_done + EACH, pieces)
        bulk_start(bulk_done, more)
        bulk_done = more
        if turn < units:
            unit = ORDER[turn]
            if unit in (phases, 2 * phases):
                widen(*((0, to_mate) if unit == phases else (1, to_cousin)))
            if phases <= unit < 2 * phases:
                more = max(relay_done, (unit - phases + 1) * parts)
                relay_start(relay_done, more)
                relay_done = more
            if unit >= phases:
                prepare(unit)
            multiply(unit)
        for lag, stage in zip(LAGS, (sum_cores, sum_far, sum_z, sum_y, pass_on)):
            if 0 <= turn - lag < units:
                stage(ORDER[turn - lag])
        more = min(max(relay_done, RELAY[7] + int(PACE * (turn + 1))), bulk_done)
        relay_start(relay_done, more)
        relay_done = more
    out[0] = final[0]

    for which in range(2):
        for part in range(phases // 2):
            swap(which, part).wait_recv()
        for chip in range(blocks // 2):
            own, far = (
                jnp.concatenate([ref[which, part, chip] for part in range(phases // 2)], axis=0)
                for ref in (xin, sin)
            )
            rows_of_chip = jnp.concatenate(
                [jnp.where(core == 0, own, far), jnp.where(core == 0, far, own)], axis=0
            ).T
            at = slice(128 * chip, 128 * chip + 128)
            out[(2 - odd) if which == 0 else (1 + odd), :, at] = final[1 + which, :, at] + jnp.where(
                core == 0, rows_of_chip[:share], rows_of_chip[share:]
            )

    arrived(pfar, pin, osem, orsem.at[0]).wait_send()
    arrived(amsg, ain, zsem, zrsem.at[0]).wait_send()
    arrived(fmsg, fin, fsem, frsem.at[0]).wait_send()
    arrived(ymsg, yin, ysem, yrsem.at[0]).wait_send()
    arrived(xin, sin, xsem, wrsem.at[0, 0]).wait_send()
    arrived(xin, sin, wsem, wrsem.at[0, 0]).wait_send()
    arrived(raw.at[0], raw.at[1], msem, mrsem.at[0]).wait_send()
    to_mate.wait_send()
    to_cousin.wait_send()


def whole(mesh, methyl, atlas, panel_ids):
    samps, probes_n = mesh.shape["samp"], mesh.shape["probe"]
    rows, cols = methyl.shape
    share, width = rows // probes_n, cols // samps
    phases = share // GROUP
    units = 3 * phases
    pieces = phases * (probes_n // PIECE)
    per_core = probes_n // 2
    vmem = pl.BlockSpec(memory_space=pltpu.VMEM)
    dma = pltpu.SemaphoreType.DMA
    return pl.pallas_call(
        functools.partial(program_kernel, samps, probes_n, rows * samps),
        out_shape=(
            jax.ShapeDtypeStruct((K, share), F32),
            jax.ShapeDtypeStruct((3, share, rows), F32),
        ),
        in_specs=[vmem] * 3,
        out_specs=(vmem,) * 2,
        scratch_shapes=[
            pltpu.VMEM((probes_n, K, 128), F32),
            pltpu.VMEM((probes_n, K, 128), F32),
            pltpu.VMEM((K, K, 128), F32),
            pltpu.VMEM((share, 4 * K), BF16),
            pltpu.VMEM((probes_n, share, 4 * K), BF16),
            pltpu.VMEM((samps, K, width + 128), F32),
            pltpu.VMEM((samps, K, width + 128), F32),
            pltpu.VMEM((K, width), F32),
            pltpu.VMEM((samps, K, width), F32),
            pltpu.VMEM((rows, cols), F32),
            pltpu.VMEM((1, cols), F32),
            pltpu.VMEM((samps, 1, cols), F32),
            pltpu.VMEM((4 * K, cols), BF16),
            pltpu.VMEM((K, rows), BF16),
            pltpu.VMEM((2, K, rows), BF16),
            pltpu.VMEM((2, probes_n, share, 4 * K), BF16),
            pltpu.VMEM((probes_n, share, cols), BF16),
            pltpu.VMEM((2, phases, probes_n, GROUP, cols // 2), BF16),
            pltpu.VMEM((units, per_core, GROUP, rows), F32),
            pltpu.VMEM((units, per_core, GROUP, rows), BF16),
            pltpu.VMEM((units, per_core, GROUP, rows), BF16),
            pltpu.VMEM((units, 2, 2, GROUP, rows), BF16),
            pltpu.VMEM((units, 2, 2, GROUP, rows), BF16),
            pltpu.VMEM((units, 2, GROUP, rows), BF16),
            pltpu.VMEM((units, 2, GROUP, rows), BF16),
            pltpu.VMEM((units, 2, GROUP, rows), F32),
            pltpu.VMEM((units, GROUP, rows), BF16),
            pltpu.VMEM((units, GROUP, rows), BF16),
            pltpu.VMEM((3, share, rows), F32),
            pltpu.VMEM((2, phases // 2, per_core, 2 * GROUP, 2 * share), F32),
            pltpu.VMEM((2, phases // 2, per_core, 2 * GROUP, 2 * share), F32),
            dma, dma, dma, dma, dma, dma, dma, dma, dma, dma,
            dma((2,)), dma((2,)), dma, dma((pieces,)), dma((pieces,)), dma((pieces,)),
            dma, dma((units,)), dma, dma((units,)), dma, dma((units,)), dma, dma((units,)),
            dma, dma((2, phases // 2)), dma, dma((2, phases // 2)),
        ],
        compiler_params=pltpu.CompilerParams(
            collective_id=0, has_side_effects=True, vmem_limit_bytes=60 * 1024 * 1024
        ),
        name="whole",
    )(methyl.reshape(probes_n, share, cols), atlas, panel_ids.reshape(1, -1))


def solution(mesh):
    def body(methyl, atlas, panel_ids):
        scores, relmat = whole(mesh, methyl, atlas, panel_ids)
        return jnp.swapaxes(relmat, 1, 2), scores

    return jax.shard_map(
        body,
        mesh=mesh,
        in_specs=(P("samp", "probe"), P(None, "probe"), P()),
        out_specs=(P(None, "samp", "probe"), P(None, ("samp", "probe"))),
        check_vma=False,
    )
```

time: 155 us -> 131 us (0.85)
  Pallas kernels: 150 us -> 127 us
    pallas_call x1, Pallas kernels: 150 us -> 127 us  [whole(): pl.pallas_call(functools.partial(program_kernel, samps, probes_n, rows *...]
where the time goes in v4:
time: 131 us
  Pallas kernels  127 us (97%)
  local copies, waits for them, and re-layouts  3.41 us (3%)
    pallas_call x1, Pallas kernels, whole(): pl.pallas_call(functools.partial(program_kernel, samps, probes_n, rows *...  127 us
    unnamed x2, local copies, waits for them, and re-layouts  3.41 us

profile of v4, /device:TPU:1, one launch (start us, length us, event | category | flops | bytes accessed | tf_op | source)
XLA Modules:
  0.0 131.2 jit_solution(674082594501188149)
XLA Ops:
  0.6 127.2 %whole.1 = (f32[32,64]{1,0:T(8,128)}, f32[3,64,1024]{2,1,0:T(8,128)}) custom-call(bf16[16,64,2048]{2,1,0:T(8,128)(2,1)} %bitcast.3, bf16[64,2048]{1,0:T(8,128)(2,1)} %atlas.1, s32[1,64]{1,0:T(1,128)} %bitcast.5), custom_call_target="tpu_custom_call" | custom-call | tf_op jit(solution)/shard_map/whole/pallas_call | solution.py:466
  127.8 2.1 %copy.7 = f32[3,1024,64]{1,2,0:T(8,128)} copy(f32[3,1024,64]{1,2,0:T(8,128)} %bitcast.4) | data formatting | bytes 1572864
  129.9 1.3 %copy.8 = f32[32,64]{1,0:T(8,128)} copy(f32[32,64]{1,0:T(8,128)} %get-tuple-element.9) | data formatting | bytes 16384

commit v5 on v4

--- a/solution.py
+++ b/solution.py
@@ -10,13 +10,13 @@
 K = 32
 ITERS = 128
 GROUP = 16
-PIECE = 4
-BULK = (3, 4, 5, 6, 8)
-RELAY = (0, 0, 0, 1, 2, 3, 4, 5)
-EACH = 2
-PACE = 2
+PIECE = 2
+BULK = (6, 9, 13, 17, 21)
+RELAY = (0, 0, 0, 2, 5, 8, 12, 15)
+EACH = 3
+PACE = 3
 LAGS = (1, 3, 5, 7, 9)
-ORDER = (0, 1, 2, 4, 3, 5, 6, 7, 8, 9, 10, 11)
+ORDER = (0, 1, 2, 3, 4, 5, 6, 7, 8, 9, 10, 11)
 MESH = pl.DeviceIdType.MESH
 F32 = jnp.float32
 BF16 = jnp.bfloat16
@@ -48,6 +48,14 @@
     copy.wait_send()
 
 
+def pack(square):
+    return jnp.concatenate([square[i * K // 4:(i + 1) * K // 4] for i in range(4)], axis=1)
+
+
+def unpack(packed):
+    return jnp.concatenate([packed[:, i * K:(i + 1) * K] for i in range(4)], axis=0)
+
+
 def split3(value):
     high = value.astype(BF16)
     rest = value - high.astype(F32)
@@ -60,7 +68,7 @@
     samps, probes_n, samples,
     methyl, atlas, ids, scores, out,
     pmsg, prcv, gcol, dmsg, drcv, cmsg, crcv, lmsg, lrcv, resid, smsg, srcv, lsplit,
-    nmsg, nrcv, near, znat, raw, pown, pfar, pin, amsg, ain, fmsg, fin, bsum, ymsg, yin, final, xin, sin,
+    nmsg, nrcv, near, znat, raw, pown, pfar, pin, amsg, ain, fmsg, fin, bsum, ymsg, yin, final, xmsg, xin, sin, own4,
     psem, prsem, dsem, drsem, csem, crsem, lsem, lrsem, ssem, srsem,
     nsem, nrsem, msem, mrsem, rsem, rrsem, osem, orsem, zsem, zrsem, fsem, frsem, ysem, yrsem, xsem, xrsem, wsem, wrsem,
 ):
@@ -101,13 +109,20 @@
     selector = select_t.T[:K].astype(BF16)
     panel = dot(selector, atlas[...]).astype(BF16)
     gram_part = dot(panel, panel, ((1,), (1,)))
-    pad = jnp.zeros((K, 128 - share - K), F32)
+    half = K // 2
+    left = lax.broadcasted_iota(jnp.int32, (half, 128), 1) < share
+    gram_rows = pack(gram_part)
 
     def project(step, carry):
         block = methyl[pl.ds(2 * step, 2)].reshape(2 * share, cols)
         part = dot(panel, block, ((1,), (1,)))
-        pmsg[2 * step] = jnp.concatenate([part[:, :share], gram_part, pad], axis=1)
-        pmsg[2 * step + 1] = jnp.concatenate([part[:, share:], gram_part, pad], axis=1)
+        top, low = part[:half], part[half:]
+        pmsg[2 * step] = jnp.concatenate(
+            [jnp.where(left, top, pltpu.roll(low, share, axis=1)), gram_rows], axis=0
+        )
+        pmsg[2 * step + 1] = jnp.concatenate(
+            [jnp.where(left, pltpu.roll(top, share, axis=1), low), gram_rows], axis=0
+        )
         return carry
     lax.fori_loop(0, probes_n // 2, project, 0)
 
@@ -153,7 +168,7 @@
     total = prcv[0]
     for peer in range(1, probes_n):
         total = total + prcv[peer]
-    gram = total[:, share:share + K]
+    gram = unpack(total[half:])
 
     diag = lax.broadcasted_iota(jnp.int32, (K, K), 0) == lax.broadcasted_iota(jnp.int32, (K, K), 1)
     trace = jnp.sum(jnp.where(diag, gram, 0.0), axis=(0, 1), keepdims=True)
@@ -161,7 +176,7 @@
     moving = jnp.where(diag, 1.0, 0.0) - gram * rate
     for k in range(K):
         gcol[k] = jnp.broadcast_to(moving[:, k:k + 1], (K, 128))
-    goal = total * rate
+    goal = jnp.concatenate([total[:half], pltpu.roll(total[:half], share, axis=1)], axis=0) * rate
 
     def descend(step, state):
         sums = [goal, None]
@@ -178,15 +193,20 @@
     weights = state[:, :share]
     scores[...] = weights * float(K)
 
-    four = jnp.concatenate([weights] * 4, axis=0)
-    wide = jnp.concatenate([four, jnp.zeros((4 * K, 128 - share), F32)], axis=1)
-    dmsg[...] = wide.T[:share].astype(BF16)
+    dmsg[...] = jnp.concatenate([weights[:half], weights[half:]], axis=1).astype(BF16)
     from_d = lambda peer: dmsg
     exchange_start(from_d, drcv, dsem, drsem, "probe", probes_n, me_p)
     drcv[me_p] = dmsg[...]
     exchange_wait(drcv, dsem, drsem, "probe", probes_n, me_p)
-    design4 = drcv[...].reshape(rows, 4 * K)
-    design = design4.astype(F32).T[:K].astype(BF16)
+    columns = []
+    for chip in range(probes_n // 2):
+        one, two = drcv[2 * chip].astype(F32), drcv[2 * chip + 1].astype(F32)
+        columns.append(jnp.concatenate([
+            jnp.where(left, one, pltpu.roll(two, share, axis=1)),
+            jnp.where(left, pltpu.roll(one, share, axis=1), two),
+        ], axis=0))
+    design_wide = jnp.concatenate(columns, axis=1)
+    design = design_wide.astype(BF16)
     nmsg[...] = design
 
     def issue(slot):
@@ -195,27 +215,28 @@
     issue(1)
 
     wgram_part = dot(design, design, ((1,), (1,)))
-    wpad = jnp.concatenate([wgram_part, jnp.zeros((K, 128 - K), F32)], axis=1)
+    wrow = jnp.concatenate([pack(wgram_part), jnp.zeros((K // 4, width - 128), F32)], axis=1)
 
     def crossing(step, carry):
         at = pl.ds(pl.multiple_of(step * width, width), width)
-        cmsg[step] = jnp.concatenate([dot(design, methyl[:, :, at].reshape(rows, width)), wpad], axis=1)
+        cmsg[step] = jnp.concatenate([dot(design, methyl[:, :, at].reshape(rows, width)), wrow], axis=0)
         return carry
     lax.fori_loop(0, samps, crossing, 0)
     from_c = lambda peer: cmsg.at[peer]
     exchange_start(from_c, crcv, csem, crsem, "samp", samps, me_s)
     crcv[me_s] = cmsg[me_s]
+    own4[...] = jnp.concatenate([design_wide] * 4, axis=0).T.astype(BF16).reshape(blocks, share, 4 * K)
     exchange_wait(crcv, csem, crsem, "samp", samps, me_s)
     issue(2)
     both = crcv[0]
     for peer in range(1, samps):
         both = both + crcv[peer]
 
-    matrix = both[:, width:]
+    matrix = jnp.concatenate([unpack(both[K:, :128]), jnp.zeros((K, 128 - K), F32)], axis=1)
     row_id = lax.broadcasted_iota(jnp.int32, (K, 128), 0)
     lane_id = lax.broadcasted_iota(jnp.int32, (K, 128), 1)
     matrix = matrix + jnp.where(row_id == lane_id, 0.0001 * samples, 0.0)
-    right = both[:, :width]
+    right = both[:K]
     row_w = lax.broadcasted_iota(jnp.int32, (K, 1), 0)
     for k in range(K):
         column = matrix[:, k:k + 1]
@@ -243,7 +264,7 @@
         sums = jnp.zeros((1, width), F32)
         for b in range(0, blocks, part_blocks):
             res = methyl[b:b + part_blocks, :, at].reshape(256, width).astype(F32) - dot(
-                drcv[b:b + part_blocks].reshape(256, 4 * K), stacked
+                own4[b:b + part_blocks].reshape(256, 4 * K), stacked
             )
             resid[b * share:b * share + 256, at] = res
             sums = sums + jnp.sum(res * res, axis=0, keepdims=True)
@@ -305,7 +326,7 @@
 
     def across(which, part, chip):
         return pltpu.make_async_remote_copy(
-            src_ref=final.at[1 + which, pl.ds(part * pair, pair), pl.ds(pl.multiple_of(chip * 128, 128), 128)],
+            src_ref=xmsg.at[which, pl.ds(part * pair, pair), pl.ds(pl.multiple_of(chip * 128, 128), 128)],
             dst_ref=xin.at[which, part, mine],
             send_sem=xsem, recv_sem=xrsem.at[which, part],
             device_id={"samp": (mate, cousin)[which], "probe": 2 * chip + core}, device_id_type=MESH,
@@ -387,6 +408,8 @@
         value = (bsum[unit, y_at] + yin[unit].astype(F32)) * (1.0 / (cols * probes_n))
         tile, phase = divmod(unit, phases)
         final[tile, phase * GROUP:(phase + 1) * GROUP] = value
+        if tile:
+            xmsg[tile - 1, phase * GROUP:(phase + 1) * GROUP] = value.astype(BF16)
         if tile and phase % 2:
             def send(step, carry):
                 across(tile - 1, phase // 2, lax.rem(mine + step, blocks // 2)).start()
@@ -402,8 +425,27 @@
 
     units = 3 * phases
 
+    def assemble(which):
+        for part in range(phases // 2):
+            swap(which, part).wait_recv()
+        for chip in range(blocks // 2):
+            own, far = (
+                jnp.concatenate([ref[which, part, chip] for part in range(phases // 2)], axis=0).astype(F32)
+                for ref in (xin, sin)
+            )
+            rows_of_chip = jnp.concatenate(
+                [jnp.where(core == 0, own, far), jnp.where(core == 0, far, own)], axis=0
+            ).T
+            at = slice(128 * chip, 128 * chip + 128)
+            out[(2 - odd) if which == 0 else (1 + odd), :, at] = final[1 + which, :, at] + jnp.where(
+                core == 0, rows_of_chip[:share], rows_of_chip[share:]
+            )
+
     bulk_done, relay_done = BULK[4], RELAY[7]
     for turn in range(units + LAGS[4]):
+        if turn == units + LAGS[4] - 2:
+            out[0] = final[0]
+            assemble(0)
         more = min(bulk_done + EACH, pieces)
         bulk_start(bulk_done, more)
         bulk_done = more
@@ -424,23 +466,7 @@
         more = min(max(relay_done, RELAY[7] + int(PACE * (turn + 1))), bulk_done)
         relay_start(relay_done, more)
         relay_done = more
-    out[0] = final[0]
-
-    for which in range(2):
-        for part in range(phases // 2):
-            swap(which, part).wait_recv()
-        for chip in range(blocks // 2):
-            own, far = (
-                jnp.concatenate([ref[which, part, chip] for part in range(phases // 2)], axis=0)
-                for ref in (xin, sin)
-            )
-            rows_of_chip = jnp.concatenate(
-                [jnp.where(core == 0, own, far), jnp.where(core == 0, far, own)], axis=0
-            ).T
-            at = slice(128 * chip, 128 * chip + 128)
-            out[(2 - odd) if which == 0 else (1 + odd), :, at] = final[1 + which, :, at] + jnp.where(
-                core == 0, rows_of_chip[:share], rows_of_chip[share:]
-            )
+    assemble(1)
 
     arrived(pfar, pin, osem, orsem.at[0]).wait_send()
     arrived(amsg, ain, zsem, zrsem.at[0]).wait_send()
@@ -472,13 +498,13 @@
         in_specs=[vmem] * 3,
         out_specs=(vmem,) * 2,
         scratch_shapes=[
-            pltpu.VMEM((probes_n, K, 128), F32),
-            pltpu.VMEM((probes_n, K, 128), F32),
+            pltpu.VMEM((probes_n, 3 * K // 4, 128), F32),
+            pltpu.VMEM((probes_n, 3 * K // 4, 128), F32),
             pltpu.VMEM((K, K, 128), F32),
-            pltpu.VMEM((share, 4 * K), BF16),
-            pltpu.VMEM((probes_n, share, 4 * K), BF16),
-            pltpu.VMEM((samps, K, width + 128), F32),
-            pltpu.VMEM((samps, K, width + 128), F32),
+            pltpu.VMEM((K // 2, 128), BF16),
+            pltpu.VMEM((probes_n, K // 2, 128), BF16),
+            pltpu.VMEM((samps, 5 * K // 4, width), F32),
+            pltpu.VMEM((samps, 5 * K // 4, width), F32),
             pltpu.VMEM((K, width), F32),
             pltpu.VMEM((samps, K, width), F32),
             pltpu.VMEM((rows, cols), F32),
@@ -501,8 +527,10 @@
             pltpu.VMEM((units, GROUP, rows), BF16),
             pltpu.VMEM((units, GROUP, rows), BF16),
             pltpu.VMEM((3, share, rows), F32),
-            pltpu.VMEM((2, phases // 2, per_core, 2 * GROUP, 2 * share), F32),
-            pltpu.VMEM((2, phases // 2, per_core, 2 * GROUP, 2 * share), F32),
+            pltpu.VMEM((2, share, rows), BF16),
+            pltpu.VMEM((2, phases // 2, per_core, 2 * GROUP, 2 * share), BF16),
+            pltpu.VMEM((2, phases // 2, per_core, 2 * GROUP, 2 * share), BF16),
+            pltpu.VMEM((probes_n, share, 4 * K), BF16),
             dma, dma, dma, dma, dma, dma, dma, dma, dma, dma,
             dma((2,)), dma((2,)), dma, dma((pieces,)), dma((pieces,)), dma((pieces,)),
             dma, dma((units,)), dma, dma((units,)), dma, dma((units,)), dma, dma((units,)),

time: 131 us -> 124 us (0.947)
  Pallas kernels: 127 us -> 120 us
    pallas_call x1, Pallas kernels: 127 us -> 120 us  [whole(): pl.pallas_call(functools.partial(program_kernel, samps, probes_n, rows *...]
where the time goes in v5:
time: 124 us
  Pallas kernels  120 us (97%)
  local copies, waits for them, and re-layouts  3.41 us (3%)
    pallas_call x1, Pallas kernels, whole(): pl.pallas_call(functools.partial(program_kernel, samps, probes_n, rows *...  120 us
    unnamed x2, local copies, waits for them, and re-layouts  3.41 us

profile of v5, /device:TPU:1, one launch (start us, length us, event | category | flops | bytes accessed | tf_op | source)
XLA Modules:
  0.0 123.9 jit_solution(10481895711461909024)
XLA Ops:
  0.6 119.8 %whole.1 = (f32[32,64]{1,0:T(8,128)}, f32[3,64,1024]{2,1,0:T(8,128)}) custom-call(bf16[16,64,2048]{2,1,0:T(8,128)(2,1)} %bitcast.3, bf16[64,2048]{1,0:T(8,128)(2,1)} %atlas.1, s32[1,64]{1,0:T(1,128)} %bitcast.5), custom_call_target="tpu_custom_call" | custom-call | tf_op jit(solution)/shard_map/whole/pallas_call | solution.py:492
  120.5 2.1 %copy.7 = f32[3,1024,64]{1,2,0:T(8,128)} copy(f32[3,1024,64]{1,2,0:T(8,128)} %bitcast.4) | data formatting | bytes 1572864
  122.5 1.3 %copy.8 = f32[32,64]{1,0:T(8,128)} copy(f32[32,64]{1,0:T(8,128)} %get-tuple-element.9) | data formatting | bytes 16384

commit v6 on v5

--- a/solution.py
+++ b/solution.py
@@ -11,11 +11,12 @@
 ITERS = 128
 GROUP = 16
 PIECE = 2
-BULK = (6, 9, 13, 17, 21)
-RELAY = (0, 0, 0, 2, 5, 8, 12, 15)
+BULK = (1, 6, 7, 10, 12, 15, 16, 19, 20, 23)
+RELAY = (0, 0, 0, 3, 6, 9, 13, 16)
 EACH = 3
 PACE = 3
 LAGS = (1, 3, 5, 7, 9)
+LAGS_OWN = (1, 3, 5, 10, 11)
 ORDER = (0, 1, 2, 3, 4, 5, 6, 7, 8, 9, 10, 11)
 MESH = pl.DeviceIdType.MESH
 F32 = jnp.float32
@@ -66,11 +67,12 @@
 
 def program_kernel(
     samps, probes_n, samples,
-    methyl, atlas, ids, scores, out,
+    methyl_in, atlas, ids, scores, out,
+    methyl,
     pmsg, prcv, gcol, dmsg, drcv, cmsg, crcv, lmsg, lrcv, resid, smsg, srcv, lsplit,
     nmsg, nrcv, near, znat, raw, pown, pfar, pin, amsg, ain, fmsg, fin, bsum, ymsg, yin, final, xmsg, xin, sin, own4,
     psem, prsem, dsem, drsem, csem, crsem, lsem, lrsem, ssem, srsem,
-    nsem, nrsem, msem, mrsem, rsem, rrsem, osem, orsem, zsem, zrsem, fsem, frsem, ysem, yrsem, xsem, xrsem, wsem, wrsem,
+    nsem, nrsem, msem, mrsem, rsem, rrsem, osem, orsem, zsem, zrsem, fsem, frsem, ysem, yrsem, xsem, xrsem, wsem, wrsem, insem,
 ):
     me_p = lax.axis_index("probe")
     me_s = lax.axis_index("samp")
@@ -104,6 +106,14 @@
     greet("samp", samps, me_s)
     greet("probe", probes_n, me_p)
 
+    quarter = blocks // 4
+
+    def fetch(part):
+        at = pl.ds(part * quarter, quarter)
+        return pltpu.make_async_copy(methyl_in.at[at], methyl.at[at], insem.at[part])
+    for part in range(4):
+        fetch(part).start()
+
     kinds = atlas.shape[0]
     select_t = (lax.broadcasted_iota(jnp.int32, (kinds, kinds), 0) == ids[...]).astype(F32)
     selector = select_t.T[:K].astype(BF16)
@@ -124,7 +134,9 @@
             [jnp.where(left, pltpu.roll(top, share, axis=1), low), gram_rows], axis=0
         )
         return carry
-    lax.fori_loop(0, probes_n // 2, project, 0)
+    for part in range(4):
+        fetch(part).wait()
+        lax.fori_loop(part * quarter // 2, (part + 1) * quarter // 2, project, 0)
 
     pl.semaphore_wait(barrier, probes_n - 1 + samps - 1)
     from_p = lambda peer: pmsg.at[peer]
@@ -163,6 +175,7 @@
             return carry
         lax.fori_loop(first, past, body, 0)
 
+    bulk_start(0, BULK[0])
     prcv[me_p] = pmsg[me_p]
     exchange_wait(prcv, psem, prsem, "probe", probes_n, me_p)
     total = prcv[0]
@@ -184,7 +197,7 @@
             term = gcol[k] * jnp.broadcast_to(state[k:k + 1, :], (K, 128))
             sums[k % 2] = term if sums[k % 2] is None else sums[k % 2] + term
         return jnp.maximum(sums[0] + sums[1], 0.0)
-    bulk_start(0, BULK[0])
+    bulk_start(BULK[0], BULK[1])
     state = jnp.full((K, 128), 1.0 / K, F32)
     for segment in range(4):
         state = lax.fori_loop(0, ITERS // 4, descend, state)
@@ -196,6 +209,7 @@
     dmsg[...] = jnp.concatenate([weights[:half], weights[half:]], axis=1).astype(BF16)
     from_d = lambda peer: dmsg
     exchange_start(from_d, drcv, dsem, drsem, "probe", probes_n, me_p)
+    bulk_start(BULK[1], BULK[2])
     drcv[me_p] = dmsg[...]
     exchange_wait(drcv, dsem, drsem, "probe", probes_n, me_p)
     columns = []
@@ -210,7 +224,7 @@
     nmsg[...] = design
 
     def issue(slot):
-        bulk_start(BULK[slot - 1], BULK[slot])
+        bulk_start(BULK[2 * slot], BULK[2 * slot + 1])
         relay_start(RELAY[slot + 2], RELAY[slot + 3])
     issue(1)
 
@@ -224,6 +238,7 @@
     lax.fori_loop(0, samps, crossing, 0)
     from_c = lambda peer: cmsg.at[peer]
     exchange_start(from_c, crcv, csem, crsem, "samp", samps, me_s)
+    bulk_start(BULK[3], BULK[4])
     crcv[me_s] = cmsg[me_s]
     own4[...] = jnp.concatenate([design_wide] * 4, axis=0).T.astype(BF16).reshape(blocks, share, 4 * K)
     exchange_wait(crcv, csem, crsem, "samp", samps, me_s)
@@ -250,6 +265,7 @@
     lmsg[...] = right / pivots
     from_l = lambda peer: lmsg
     exchange_start(from_l, lrcv, lsem, lrsem, "samp", samps, me_s)
+    bulk_start(BULK[5], BULK[6])
     lrcv[me_s] = lmsg[...]
     exchange_wait(lrcv, lsem, lrsem, "samp", samps, me_s)
 
@@ -273,12 +289,12 @@
     lax.fori_loop(0, samps, residue, 0)
     from_s = lambda peer: smsg
     exchange_start(from_s, srcv, ssem, srsem, "samp", samps, me_s)
+    bulk_start(BULK[7], BULK[8])
     srcv[me_s] = smsg[...]
     exchange_wait(srcv, ssem, srsem, "samp", samps, me_s)
     to_mate = copy_to(nmsg, nrcv.at[0], nsem.at[0], nrsem.at[0], "samp", mate)
-    to_cousin = copy_to(nmsg, nrcv.at[1], nsem.at[1], nrsem.at[1], "samp", cousin)
+    to_cousin = copy_to(nrcv.at[0], nrcv.at[1], nsem.at[1], nrsem.at[1], "samp", onward)
     to_mate.start()
-    to_cousin.start()
     issue(4)
     spread = srcv[0]
     for peer in range(1, samps):
@@ -296,6 +312,8 @@
 
     def widen(which, copy):
         copy.wait_recv()
+        if which == 0:
+            to_cousin.start()
         others = nrcv[which].astype(F32)
         near[which] = jnp.concatenate([others] * 4, axis=0).T.astype(BF16).reshape(blocks, share, 4 * K)
 
@@ -441,7 +459,7 @@
                 core == 0, rows_of_chip[:share], rows_of_chip[share:]
             )
 
-    bulk_done, relay_done = BULK[4], RELAY[7]
+    bulk_done, relay_done = BULK[9], RELAY[7]
     for turn in range(units + LAGS[4]):
         if turn == units + LAGS[4] - 2:
             out[0] = final[0]
@@ -460,9 +478,10 @@
             if unit >= phases:
                 prepare(unit)
             multiply(unit)
-        for lag, stage in zip(LAGS, (sum_cores, sum_far, sum_z, sum_y, pass_on)):
-            if 0 <= turn - lag < units:
-                stage(ORDER[turn - lag])
+        for number, stage in enumerate((sum_cores, sum_far, sum_z, sum_y, pass_on)):
+            for spot, unit in enumerate(ORDER):
+                if turn - spot == (LAGS_OWN if unit < phases else LAGS)[number]:
+                    stage(unit)
         more = min(max(relay_done, RELAY[7] + int(PACE * (turn + 1))), bulk_done)
         relay_start(relay_done, more)
         relay_done = more
@@ -495,9 +514,10 @@
             jax.ShapeDtypeStruct((K, share), F32),
             jax.ShapeDtypeStruct((3, share, rows), F32),
         ),
-        in_specs=[vmem] * 3,
+        in_specs=[pl.BlockSpec(memory_space=pl.ANY), vmem, vmem],
         out_specs=(vmem,) * 2,
         scratch_shapes=[
+            pltpu.VMEM((probes_n, share, cols), BF16),
             pltpu.VMEM((probes_n, 3 * K // 4, 128), F32),
             pltpu.VMEM((probes_n, 3 * K // 4, 128), F32),
             pltpu.VMEM((K, K, 128), F32),
@@ -534,7 +554,7 @@
             dma, dma, dma, dma, dma, dma, dma, dma, dma, dma,
             dma((2,)), dma((2,)), dma, dma((pieces,)), dma((pieces,)), dma((pieces,)),
             dma, dma((units,)), dma, dma((units,)), dma, dma((units,)), dma, dma((units,)),
-            dma, dma((2, phases // 2)), dma, dma((2, phases // 2)),
+            dma, dma((2, phases // 2)), dma, dma((2, phases // 2)), dma((4,)),
         ],
         compiler_params=pltpu.CompilerParams(
             collective_id=0, has_side_effects=True, vmem_limit_bytes=60 * 1024 * 1024

time: 124 us -> 121 us (0.976)
  Pallas kernels: 120 us -> 116 us
    pallas_call x1, Pallas kernels: 120 us -> 116 us  [whole(): pl.pallas_call(functools.partial(program_kernel, samps, probes_n, rows *...]
where the time goes in v6:
time: 121 us; the launch traced here: 120 us
  Pallas kernels  116 us (96%)
  local copies, waits for them, and re-layouts  3.41 us (3%)
    pallas_call x1, Pallas kernels, whole(): pl.pallas_call(functools.partial(program_kernel, samps, probes_n, rows *...  116 us
    unnamed x2, local copies, waits for them, and re-layouts  3.41 us

profile of v6, /device:TPU:1, one launch (start us, length us, event | category | flops | bytes accessed | tf_op | source)
XLA Modules:
  0.0 120.4 jit_solution(15788393514267171300)
XLA Ops:
  0.6 116.4 %whole.1 = (f32[32,64]{1,0:T(8,128)}, f32[3,64,1024]{2,1,0:T(8,128)}) custom-call(bf16[16,64,2048]{2,1,0:T(8,128)(2,1)} %bitcast.3, bf16[64,2048]{1,0:T(8,128)(2,1)} %atlas.1, s32[1,64]{1,0:T(1,128)} %bitcast.5), custom_call_target="tpu_custom_call" | custom-call | tf_op jit(solution)/shard_map/whole/pallas_call | solution.py:511
  117.0 2.1 %copy.7 = f32[3,1024,64]{1,2,0:T(8,128)} copy(f32[3,1024,64]{1,2,0:T(8,128)} %bitcast.4) | data formatting | bytes 1572864
  119.1 1.3 %copy.8 = f32[32,64]{1,0:T(8,128)} copy(f32[32,64]{1,0:T(8,128)} %get-tuple-element.9) | data formatting | bytes 16384

commit v7 on v6

--- a/solution.py
+++ b/solution.py
@@ -11,7 +11,7 @@
 ITERS = 128
 GROUP = 16
 PIECE = 2
-BULK = (1, 6, 7, 10, 12, 15, 16, 19, 20, 23)
+BULK = (1, 6, 7, 10, 12, 15, 17, 20, 22, 25)
 RELAY = (0, 0, 0, 3, 6, 9, 13, 16)
 EACH = 3
 PACE = 3

time: 121 us -> 122 us (level)
  no operation moved by 1% of the time
where the time goes in v7:
time: 122 us; the launch traced here: 121 us
  Pallas kernels  117 us (96%)
  local copies, waits for them, and re-layouts  3.41 us (3%)
    pallas_call x1, Pallas kernels, whole(): pl.pallas_call(functools.partial(program_kernel, samps, probes_n, rows *...  117 us
    unnamed x2, local copies, waits for them, and re-layouts  3.41 us

profile of v7, /device:TPU:1, one launch (start us, length us, event | category | flops | bytes accessed | tf_op | source)
XLA Modules:
  0.0 121.3 jit_solution(18417788219117324412)
XLA Ops:
  0.6 117.3 %whole.1 = (f32[32,64]{1,0:T(8,128)}, f32[3,64,1024]{2,1,0:T(8,128)}) custom-call(bf16[16,64,2048]{2,1,0:T(8,128)(2,1)} %bitcast.3, bf16[64,2048]{1,0:T(8,128)(2,1)} %atlas.1, s32[1,64]{1,0:T(1,128)} %bitcast.5), custom_call_target="tpu_custom_call" | custom-call | tf_op jit(solution)/shard_map/whole/pallas_call | solution.py:511
  117.9 2.1 %copy.7 = f32[3,1024,64]{1,2,0:T(8,128)} copy(f32[3,1024,64]{1,2,0:T(8,128)} %bitcast.4) | data formatting | bytes 1572864
  120.0 1.3 %copy.8 = f32[32,64]{1,0:T(8,128)} copy(f32[32,64]{1,0:T(8,128)} %get-tuple-element.9) | data formatting | bytes 16384
